TPU v7x, 32 devices: a whole 2x2x4 slice. The times are simulated.
32 devices in a mesh: groups: 2 (over x), seq: 16 (over z, y, core).
Axes of the slice: x: 2, y: 2, z: 4, core: 2. Of those that a mesh axis runs over, the one named last changes fastest.
Arguments:
- queries: bfloat16 [4096, 2560], P(('groups', 'seq')), parts along dimension 0, may hold values from -12 to 12
- key_vectors: bfloat16 [4096, 2560], P(('groups', 'seq')), parts along dimension 0, may hold values from -6 to 6
- value_vectors: bfloat16 [4096, 2560], P(('groups', 'seq')), parts along dimension 0, may hold values from -6 to 6
- step_sizes: float32 [4096, 8], P(('groups', 'seq')), parts along dimension 0, may hold values from 0.02 to 0.3
- fast_weights: float32 [320, 7680], P('seq'), may hold values from -20 to 20
- fast_gain: float32 [2560], replicated, may hold values from 0.25 to 1.75
- window_gain: float32 [2560], replicated, may hold values from 0.25 to 1.75
Outputs:
- layer_out: bfloat16 [4096, 2560], P(('groups', 'seq')), parts along dimension 0
- new_weights: float32 [640, 7680], P(('groups', 'seq')), parts along dimension 0
- momentum: float32 [640, 7680], P(('groups', 'seq')), parts along dimension 0
There are 2 independent parts, one for each index of `groups`. A program takes and returns all parts, laid end to end along the dimension named above; an argument that names none is the same for every part. Nothing has to cross between parts.
All inputs are finite; a program needn't handle non-finite values.
Results may differ from a plain program's by a relative error of at most 0.0066.
Values may be sent and summed in bfloat16 or wider, within the bound.
A program may use at most 128 MiB of HBM per device.

v0:
```python
import math

import jax
import jax.numpy as jnp
from jax import lax
from jax.sharding import PartitionSpec as P

WINDOW = 1024


def from_behind(value, axis, steps):
    count = lax.axis_size(axis)
    first, last = (max(0, -steps), min(count, count - steps))
    return lax.ppermute(value, axis, [(source, source + steps) for source in range(first, last)])


def normalize(field, gain_row):
    mean_sq = jnp.mean(field * field, axis=-1, keepdims=True)
    return field * lax.rsqrt(mean_sq + 1e-05) * gain_row


def silu_slope(gate):
    sigma = jax.nn.sigmoid(gate)
    return sigma * (1.0 + gate * (1.0 - sigma))


def shards(queries, key_vectors, value_vectors, step_sizes, fast_weights, fast_gain, window_gain):
    row_count = queries.shape[0]
    head_count = step_sizes.shape[1]
    head_width = queries.shape[1] // head_count
    score_scale = 1.0 / math.sqrt(head_width)
    my_place = lax.axis_index("seq")
    copies = lax.all_gather(fast_weights.astype(jnp.bfloat16), "seq", axis=0, tiled=True)
    copies = copies.reshape(head_width, 3, head_count, head_width)
    w_first = copies[:, 0]
    w_third = copies[:, 1]
    w_second = copies[:, 2]
    query_heads = queries.reshape(row_count, head_count, head_width)
    key_heads = key_vectors.reshape(row_count, head_count, head_width)
    value_heads = value_vectors.reshape(row_count, head_count, head_width)

    def project(inputs, matrix):
        return (
            jnp.einsum("thr,rhc->thc", inputs, matrix, preferred_element_type=jnp.float32)
            * score_scale
        )

    gate_query = project(query_heads, w_first)
    up_query = project(query_heads, w_third)
    hidden_query = (jax.nn.silu(gate_query) * up_query).astype(jnp.bfloat16)
    fast_part = normalize(
        project(hidden_query, w_second), fast_gain.reshape(head_count, head_width)
    )
    reach_blocks = WINDOW // row_count
    earlier = []
    carried = (key_vectors, value_vectors)
    for offset in range(reach_blocks):
        carried = from_behind((carried[0], carried[1]), "seq", 1)
        earlier = [carried] + earlier
    window_keys = jnp.concatenate([shifted[0] for shifted in earlier] + [key_vectors], axis=0)
    window_values = jnp.concatenate([shifted[1] for shifted in earlier] + [value_vectors], axis=0)
    window_keys = window_keys.reshape(-1, head_count, head_width)
    window_values = window_values.reshape(-1, head_count, head_width)
    query_pos = jnp.arange(row_count, dtype=jnp.int32)[:, None] + reach_blocks * row_count
    key_pos = jnp.arange((reach_blocks + 1) * row_count, dtype=jnp.int32)[None, :]
    distance = query_pos - key_pos
    first_key = (my_place - reach_blocks) * row_count
    allowed = (distance >= 0) & (distance < WINDOW) & (key_pos + first_key >= 0)
    scores = (
        jnp.einsum("qhd,khd->hqk", query_heads, window_keys, preferred_element_type=jnp.float32)
        * score_scale
    )
    scores = jnp.where(allowed[None], scores, -jnp.inf)
    row_max = jnp.max(scores, axis=-1, keepdims=True)
    weights = jnp.exp(scores - row_max)
    attention_probs = (weights / jnp.sum(weights, axis=-1, keepdims=True)).astype(jnp.bfloat16)
    attended = jnp.einsum(
        "hqk,khd->qhd", attention_probs, window_values, preferred_element_type=jnp.float32
    )
    window_part = normalize(attended, window_gain.reshape(head_count, head_width))
    layer_out = (
        (fast_part + window_part).astype(jnp.bfloat16).reshape(row_count, head_count * head_width)
    )
    gate_key = project(key_heads, w_first)
    up_key = project(key_heads, w_third)
    hidden_key = (jax.nn.silu(gate_key) * up_key).astype(jnp.bfloat16)
    target = (-step_sizes[:, :, None] * value_heads.astype(jnp.float32)).astype(jnp.bfloat16)
    back_hidden = (
        jnp.einsum("thc,rhc->thr", target, w_second, preferred_element_type=jnp.float32)
        * score_scale
    )
    grad_gate = (back_hidden * up_key * silu_slope(gate_key)).astype(jnp.bfloat16)
    grad_up = (back_hidden * jax.nn.silu(gate_key)).astype(jnp.bfloat16)
    first = jnp.einsum("thr,thc->rhc", key_heads, grad_gate, preferred_element_type=jnp.float32)
    third = jnp.einsum("thr,thc->rhc", key_heads, grad_up, preferred_element_type=jnp.float32)
    second = jnp.einsum("thr,thc->rhc", hidden_key, target, preferred_element_type=jnp.float32)
    gradient = jnp.stack([first, third, second], axis=1).reshape(head_width, -1) * score_scale
    momentum = lax.psum_scatter(gradient, "seq", scatter_dimension=0, tiled=True)
    moved = fast_weights - momentum
    old_sum, new_sum = lax.psum(
        (jnp.sum(fast_weights * fast_weights, axis=0), jnp.sum(moved * moved, axis=0)), "seq"
    )
    new_weights = moved * jnp.sqrt((old_sum + 1e-06) / (new_sum + 1e-06))
    return (layer_out, new_weights, momentum)


def solution(mesh):
    in_specs = (
        P(("groups", "seq"), None),
        P(("groups", "seq"), None),
        P(("groups", "seq"), None),
        P(("groups", "seq"), None),
        P("seq", None),
        P(),
        P(),
    )
    out_specs = (P(("groups", "seq"), None), P(("groups", "seq"), None), P(("groups", "seq"), None))
    return jax.shard_map(shards, mesh=mesh, in_specs=in_specs, out_specs=out_specs, check_vma=False)
```

profile of v0, /device:TPU:0, one launch (start us, length us, event | category | flops | bytes accessed | tf_op | source)
XLA Modules:
  0.0 501.7 jit_solution(17470583284559178395)
XLA Ops:
  9.8 4.5 collective-permute-start.8
  14.4 7.8 %collective-permute-start.1 = (bf16[128,2560]{1,0:T(8,128)(2,1)S(1)}, bf16[128,2560]{1,0:T(8,128)(2,1)S(1)}, u32[]{:S(2)}, u32[]{:S(2)}) collective-permute-start(bf16[128,2560]{1,0:T(8,128)(2,1)S(1)} %collective-permute-done), channel_id=1, source_target_pairs={{0,1},{1,2},{2,3},{3,4},{4,5},{5,6},{6,7},{7,8},{8,9},{9,10},{10,1... | collective-permute-start | bytes 1966088 | tf_op jit(solution)/shard_map/ppermute | solution.py:14
  22.2 7.0 %collective-permute-start.9 = (bf16[128,2560]{1,0:T(8,128)(2,1)S(1)}, bf16[128,2560]{1,0:T(8,128)(2,1)S(1)}, u32[]{:S(2)}, u32[]{:S(2)}) collective-permute-start(bf16[128,2560]{1,0:T(8,128)(2,1)S(1)} %collective-permute-done.8), channel_id=1, source_target_pairs={{0,1},{1,2},{2,3},{3,4},{4,5},{5,6},{6,7},{7,8},{8,9},{9,10},{10,1... | collective-permute-start | bytes 1966088 | tf_op jit(solution)/shard_map/ppermute | solution.py:14
  29.2 6.9 %collective-permute-start.2 = (bf16[128,2560]{1,0:T(8,128)(2,1)S(1)}, bf16[128,2560]{1,0:T(8,128)(2,1)S(1)}, u32[]{:S(2)}, u32[]{:S(2)}) collective-permute-start(bf16[128,2560]{1,0:T(8,128)(2,1)S(1)} %collective-permute-done.1), channel_id=1, source_target_pairs={{0,1},{1,2},{2,3},{3,4},{4,5},{5,6},{6,7},{7,8},{8,9},{9,10},{10,1... | collective-permute-start | bytes 1966088 | tf_op jit(solution)/shard_map/ppermute | solution.py:14
  37.0 7.0 %collective-permute-start.10 = (bf16[128,2560]{1,0:T(8,128)(2,1)S(1)}, bf16[128,2560]{1,0:T(8,128)(2,1)S(1)}, u32[]{:S(2)}, u32[]{:S(2)}) collective-permute-start(bf16[128,2560]{1,0:T(8,128)(2,1)S(1)} %collective-permute-done.9), channel_id=1, source_target_pairs={{0,1},{1,2},{2,3},{3,4},{4,5},{5,6},{6,7},{7,8},{8,9},{9,10},{10,1... | collective-permute-start | bytes 1966088 | tf_op jit(solution)/shard_map/ppermute | solution.py:14
  44.0 6.1 %collective-permute-start.3 = (bf16[128,2560]{1,0:T(8,128)(2,1)S(1)}, bf16[128,2560]{1,0:T(8,128)(2,1)S(1)}, u32[]{:S(2)}, u32[]{:S(2)}) collective-permute-start(bf16[128,2560]{1,0:T(8,128)(2,1)S(1)} %collective-permute-done.2), channel_id=1, source_target_pairs={{0,1},{1,2},{2,3},{3,4},{4,5},{5,6},{6,7},{7,8},{8,9},{9,10},{10,1... | collective-permute-start | bytes 1966088 | tf_op jit(solution)/shard_map/ppermute | solution.py:14
  50.2 7.0 %collective-permute-start.11 = (bf16[128,2560]{1,0:T(8,128)(2,1)S(1)}, bf16[128,2560]{1,0:T(8,128)(2,1)S(1)}, u32[]{:S(2)}, u32[]{:S(2)}) collective-permute-start(bf16[128,2560]{1,0:T(8,128)(2,1)S(1)} %collective-permute-done.10), channel_id=1, source_target_pairs={{0,1},{1,2},{2,3},{3,4},{4,5},{5,6},{6,7},{7,8},{8,9},{9,10},{10,1... | collective-permute-start | bytes 1966088 | tf_op jit(solution)/shard_map/ppermute | solution.py:14
  57.2 7.0 %collective-permute-start.4 = (bf16[128,2560]{1,0:T(8,128)(2,1)S(1)}, bf16[128,2560]{1,0:T(8,128)(2,1)S(1)}, u32[]{:S(2)}, u32[]{:S(2)}) collective-permute-start(bf16[128,2560]{1,0:T(8,128)(2,1)S(1)} %collective-permute-done.3), channel_id=1, source_target_pairs={{0,1},{1,2},{2,3},{3,4},{4,5},{5,6},{6,7},{7,8},{8,9},{9,10},{10,1... | collective-permute-start | bytes 1966088 | tf_op jit(solution)/shard_map/ppermute | solution.py:14
  64.2 7.8 %collective-permute-start.12 = (bf16[128,2560]{1,0:T(8,128)(2,1)S(1)}, bf16[128,2560]{1,0:T(8,128)(2,1)}, u32[]{:S(2)}, u32[]{:S(2)}) collective-permute-start(bf16[128,2560]{1,0:T(8,128)(2,1)S(1)} %collective-permute-done.11), channel_id=1, source_target_pairs={{0,1},{1,2},{2,3},{3,4},{4,5},{5,6},{6,7},{7,8},{8,9},{9,10},{10,1... | collective-permute-start | bytes 1966088 | tf_op jit(solution)/shard_map/ppermute | solution.py:14
  72.0 7.0 %collective-permute-start.5 = (bf16[128,2560]{1,0:T(8,128)(2,1)S(1)}, bf16[128,2560]{1,0:T(8,128)(2,1)}, u32[]{:S(2)}, u32[]{:S(2)}) collective-permute-start(bf16[128,2560]{1,0:T(8,128)(2,1)S(1)} %collective-permute-done.4), channel_id=1, source_target_pairs={{0,1},{1,2},{2,3},{3,4},{4,5},{5,6},{6,7},{7,8},{8,9},{9,10},{10,1... | collective-permute-start | bytes 1966088 | tf_op jit(solution)/shard_map/ppermute | solution.py:14
  81.2 4.8 collective-permute-start.13
  86.0 7.1 %collective-permute-start.6 = (bf16[128,2560]{1,0:T(8,128)(2,1)}, bf16[128,2560]{1,0:T(8,128)(2,1)}, u32[]{:S(2)}, u32[]{:S(2)}) collective-permute-start(bf16[128,2560]{1,0:T(8,128)(2,1)} %collective-permute-done.5), channel_id=1, source_target_pairs={{0,1},{1,2},{2,3},{3,4},{4,5},{5,6},{6,7},{7,8},{8,9},{9,10},{10,1... | collective-permute-start | bytes 1966088 | tf_op jit(solution)/shard_map/ppermute | solution.py:14
  97.3 6.8 %collective-permute-start.14 = (bf16[128,2560]{1,0:T(8,128)(2,1)}, bf16[128,2560]{1,0:T(8,128)(2,1)}, u32[]{:S(2)}, u32[]{:S(2)}) collective-permute-start(bf16[128,2560]{1,0:T(8,128)(2,1)} %collective-permute-done.13), channel_id=1, source_target_pairs={{0,1},{1,2},{2,3},{3,4},{4,5},{5,6},{6,7},{7,8},{8,9},{9,10},{10,1... | collective-permute-start | bytes 1966088 | tf_op jit(solution)/shard_map/ppermute | solution.py:14
  104.2 6.2 %collective-permute-start.7 = (bf16[128,2560]{1,0:T(8,128)(2,1)}, bf16[128,2560]{1,0:T(8,128)(2,1)S(1)}, u32[]{:S(2)}, u32[]{:S(2)}) collective-permute-start(bf16[128,2560]{1,0:T(8,128)(2,1)} %collective-permute-done.6), channel_id=1, source_target_pairs={{0,1},{1,2},{2,3},{3,4},{4,5},{5,6},{6,7},{7,8},{8,9},{9,10},{10,1... | collective-permute-start | bytes 1966088 | tf_op jit(solution)/shard_map/ppermute | solution.py:14
  110.6 7.6 %collective-permute-start.15 = (bf16[128,2560]{1,0:T(8,128)(2,1)}, bf16[128,2560]{1,0:T(8,128)(2,1)}, u32[]{:S(2)}, u32[]{:S(2)}) collective-permute-start(bf16[128,2560]{1,0:T(8,128)(2,1)} %collective-permute-done.14), channel_id=1, source_target_pairs={{0,1},{1,2},{2,3},{3,4},{4,5},{5,6},{6,7},{7,8},{8,9},{9,10},{10,1... | collective-permute-start | bytes 1966088 | tf_op jit(solution)/shard_map/ppermute | solution.py:14
  128.6 9.0 %copy.40 = bf16[1152,2560]{0,1:T(8,128)(2,1)} copy(bf16[1152,2560]{1,0:T(8,128)(2,1)} %constant_dynamic-update-slice_fusion) | data formatting | bytes 11796480 | tf_op jit(solution)/shard_map/concatenate | solution.py:61
  150.2 8.9 %copy.41 = bf16[1152,2560]{0,1:T(8,128)(2,1)} copy(bf16[1152,2560]{1,0:T(8,128)(2,1)} %constant_dynamic-update-slice_fusion.9) | data formatting | bytes 11796480 | tf_op jit(solution)/shard_map/concatenate | solution.py:60
  159.1 4.8 convolution_multiply_fusion
  166.0 7.1 %multiply_reduce_fusion = (f32[128,8]{0,1:T(8,128)S(1)}, f32[128,8,320]{0,2,1:T(8,128)}) fusion(bf16[1152,8,320]{0,2,1:T(8,128)(2,1)} %bitcast.127, f32[8,128]{1,0:T(8,128)S(1)} %exponential_reduce_fusion, f32[8,1152,128]{2,1,0:T(8,128)} %copy-done.4, pred[128,1152]{0,1:T(8,128)(4,1)S(1)} %fusion.69), kind=kOutput, calls=%fused_computation.48 | convolution fusion | flops 760349824 | bytes 12083200 | tf_op jit(solution)/shard_map/hqk,khd->qhd/dot_general | solution.py:77
  173.1 9.3 %reshape.102 = bf16[320,3,8,320]{3,2,1,0:T(8,128)(2,1)} reshape(bf16[16,20,7680]{2,1,0:T(8,128)(2,1)} %all-gather.3.cloned.1.call-done) | data formatting | bytes 9830400 | tf_op jit(solution)/shard_map/reshape | solution.py:34
  182.4 5.2 %fusion.82 = (bf16[320,1,8,320]{3,2,1,0:T(8,128)(2,1)}, bf16[320,1,8,320]{3,2,1,0:T(8,128)(2,1)}, bf16[320,1,8,320]{3,2,1,0:T(8,128)(2,1)S(1)}) fusion(bf16[320,3,8,320]{3,2,1,0:T(8,128)(2,1)} %reshape.102), kind=kLoop, calls=%fused_computation.93 | loop fusion | bytes 9830400 | tf_op jit(solution)/shard_map/slice | solution.py:35
  190.4 3.1 copy.51
  195.3 4.1 copy.50
  205.6 5.3 %maximum_multiply_fusion = f32[320,3,8,320]{0,3,2,1:T(8,128)} fusion(f32[320,1,8,320]{0,3,2,1:T(8,128)S(1)} %convolution_bitcast_fusion, f32[320,1,8,320]{0,3,2,1:T(8,128)S(1)} %convolution_bitcast_fusion.1, f32[320,1,8,320]{0,3,2,1:T(8,128)S(1)} %convolution_bitcast_fusion.2), kind=kLoop, calls=%fused_computation.1 | loop fusion | flops 7372800 | bytes 19660800 | tf_op jit(solution)/shard_map/mul | solution.py:97
  210.9 11.7 %copy.46 = f32[320,7680]{1,0:T(8,128)} copy(f32[320,7680]{0,1:T(8,128)} %bitcast.116) | data formatting | bytes 19660800 | tf_op jit(solution)/shard_map/mul | solution.py:97
  222.6 138.9 %fusion = f32[24,7680]{1,0:T(8,128)} fusion(f32[320,7680]{1,0:T(8,128)} %copy.46), kind=kCustom, calls=%all-reduce-scatter | all-reduce-scatter fusion | flops 2949121 | bytes 10568192
  361.5 19.8 %collective-permute-start.17 = (f32[24,7680]{1,0:T(8,128)}, f32[24,7680]{1,0:T(8,128)}, u32[]{:S(2)}, u32[]{:S(2)}) collective-permute-start(f32[24,7680]{1,0:T(8,128)} %fusion), channel_id=1, source_target_pairs={{0,2},{1,3},{2,4},{3,5},{4,6},{5,7},{6,8},{7,9},{8,10},{9,11},{10,... | collective-permute-start | bytes 2211848
  383.5 4.2 multiply_reduce_fusion.1
  388.8 14.1 %collective-permute-start.18 = (f32[12,7680]{1,0:T(8,128)S(1)}, f32[12,7680]{1,0:T(8,128)S(1)}, u32[]{:S(2)}, u32[]{:S(2)}) collective-permute-start(f32[12,7680]{1,0:T(8,128)S(1)} %slice.15), channel_id=1, source_target_pairs={{0,3},{1,4},{2,5},{3,6},{4,7},{5,8},{6,9},{7,10},{8,11},{9,12},{10... | collective-permute-start | bytes 1105928
  406.3 2.9 collective-permute-done.18
  410.0 7.8 %concatenate.8 = f32[84,7680]{1,0:T(8,128)S(1)} concatenate(f32[12,7680]{1,0:T(8,128)} %copy-done.24, f32[24,7680]{1,0:T(8,128)} %collective-permute-done.17, f32[24,7680]{1,0:T(8,128)} %collective-permute-done.16, f32[24,7680]{1,0:T(8,128)S(1)} %copy-done.3), dimensions={0} | concatenate | bytes 5160960
  419.9 74.0 %all-reduce.2 = (f32[7680]{0:T(1024)S(1)}, f32[7680]{0:T(1024)S(1)}) all-reduce(f32[7680]{0:T(1024)S(1)} %get-tuple-element.14, f32[7680]{0:T(1024)S(1)} %get-tuple-element.20), channel_id=1, replica_groups=mesh['groups'=2,'seq'=16] {'seq'}, use_global_device_ids=true, to_apply=%region_8.9 | all-reduce | flops 15360 | bytes 122880 | tf_op jit(solution)/shard_map/psum | solution.py:100
  (126 shorter events, 55.7 us)
Async XLA Ops:
  7.2 87.4 %copy-start.5 = (bf16[128,2560]{1,0:T(8,128)(2,1)S(1)}, bf16[128,2560]{1,0:T(8,128)(2,1)}, u32[]{:S(2)}) copy-start(bf16[128,2560]{1,0:T(8,128)(2,1)} %param.9) | copy-start | bytes 1966084
  7.2 88.5 %copy-start.7 = (bf16[128,2560]{1,0:T(8,128)(2,1)S(1)}, bf16[128,2560]{1,0:T(8,128)(2,1)}, u32[]{:S(2)}) copy-start(bf16[128,2560]{1,0:T(8,128)(2,1)} %param.7) | copy-start | bytes 1966084
  7.2 165.9 %all-gather.3.cloned.1.call-start = ((), (), s32[]{:S(2)}) async-start(), calls=%async_computation | async-start | bytes 6266880 | tf_op jit(solution)/shard_map/all_gather | solution.py:33
  7.2 7.1 %collective-permute-start = (bf16[128,2560]{1,0:T(8,128)(2,1)}, bf16[128,2560]{1,0:T(8,128)(2,1)S(1)}, u32[]{:S(2)}, u32[]{:S(2)}) collective-permute-start(bf16[128,2560]{1,0:T(8,128)(2,1)} %param.9), channel_id=1, source_target_pairs={{0,1},{1,2},{2,3},{3,4},{4,5},{5,6},{6,7},{7,8},{8,9},{9,10},{10,1... | collective-permute-start | bytes 1966088 | tf_op jit(solution)/shard_map/ppermute | solution.py:14
  9.8 12.4 %collective-permute-start.8 = (bf16[128,2560]{1,0:T(8,128)(2,1)}, bf16[128,2560]{1,0:T(8,128)(2,1)S(1)}, u32[]{:S(2)}, u32[]{:S(2)}) collective-permute-start(bf16[128,2560]{1,0:T(8,128)(2,1)} %param.8), channel_id=1, source_target_pairs={{0,1},{1,2},{2,3},{3,4},{4,5},{5,6},{6,7},{7,8},{8,9},{9,10},{10,1... | collective-permute-start | bytes 1966088 | tf_op jit(solution)/shard_map/ppermute | solution.py:14
  14.4 35.8 %copy-start.10 = (bf16[128,2560]{1,0:T(8,128)(2,1)}, bf16[128,2560]{1,0:T(8,128)(2,1)S(1)}, u32[]{:S(2)}) copy-start(bf16[128,2560]{1,0:T(8,128)(2,1)S(1)} %collective-permute-done) | copy-start | bytes 1966084
  14.4 14.8 %collective-permute-start.1 = (bf16[128,2560]{1,0:T(8,128)(2,1)S(1)}, bf16[128,2560]{1,0:T(8,128)(2,1)S(1)}, u32[]{:S(2)}, u32[]{:S(2)}) collective-permute-start(bf16[128,2560]{1,0:T(8,128)(2,1)S(1)} %collective-permute-done), channel_id=1, source_target_pairs={{0,1},{1,2},{2,3},{3,4},{4,5},{5,6},{6,7},{7,8},{8,9},{9,10},{10,1... | collective-permute-start | bytes 1966088 | tf_op jit(solution)/shard_map/ppermute | solution.py:14
  22.2 13.9 %collective-permute-start.9 = (bf16[128,2560]{1,0:T(8,128)(2,1)S(1)}, bf16[128,2560]{1,0:T(8,128)(2,1)S(1)}, u32[]{:S(2)}, u32[]{:S(2)}) collective-permute-start(bf16[128,2560]{1,0:T(8,128)(2,1)S(1)} %collective-permute-done.8), channel_id=1, source_target_pairs={{0,1},{1,2},{2,3},{3,4},{4,5},{5,6},{6,7},{7,8},{8,9},{9,10},{10,1... | collective-permute-start | bytes 1966088 | tf_op jit(solution)/shard_map/ppermute | solution.py:14
  29.2 35.0 %copy-start.14 = (bf16[128,2560]{1,0:T(8,128)(2,1)}, bf16[128,2560]{1,0:T(8,128)(2,1)S(1)}, u32[]{:S(2)}) copy-start(bf16[128,2560]{1,0:T(8,128)(2,1)S(1)} %collective-permute-done.1) | copy-start | bytes 1966084
  29.2 14.8 %collective-permute-start.2 = (bf16[128,2560]{1,0:T(8,128)(2,1)S(1)}, bf16[128,2560]{1,0:T(8,128)(2,1)S(1)}, u32[]{:S(2)}, u32[]{:S(2)}) collective-permute-start(bf16[128,2560]{1,0:T(8,128)(2,1)S(1)} %collective-permute-done.1), channel_id=1, source_target_pairs={{0,1},{1,2},{2,3},{3,4},{4,5},{5,6},{6,7},{7,8},{8,9},{9,10},{10,1... | collective-permute-start | bytes 1966088 | tf_op jit(solution)/shard_map/ppermute | solution.py:14
  37.0 13.2 %collective-permute-start.10 = (bf16[128,2560]{1,0:T(8,128)(2,1)S(1)}, bf16[128,2560]{1,0:T(8,128)(2,1)S(1)}, u32[]{:S(2)}, u32[]{:S(2)}) collective-permute-start(bf16[128,2560]{1,0:T(8,128)(2,1)S(1)} %collective-permute-done.9), channel_id=1, source_target_pairs={{0,1},{1,2},{2,3},{3,4},{4,5},{5,6},{6,7},{7,8},{8,9},{9,10},{10,1... | collective-permute-start | bytes 1966088 | tf_op jit(solution)/shard_map/ppermute | solution.py:14
  44.0 28.0 %copy-start.18 = (bf16[128,2560]{1,0:T(8,128)(2,1)}, bf16[128,2560]{1,0:T(8,128)(2,1)S(1)}, u32[]{:S(2)}) copy-start(bf16[128,2560]{1,0:T(8,128)(2,1)S(1)} %collective-permute-done.2) | copy-start | bytes 1966084
  44.0 13.2 %collective-permute-start.3 = (bf16[128,2560]{1,0:T(8,128)(2,1)S(1)}, bf16[128,2560]{1,0:T(8,128)(2,1)S(1)}, u32[]{:S(2)}, u32[]{:S(2)}) collective-permute-start(bf16[128,2560]{1,0:T(8,128)(2,1)S(1)} %collective-permute-done.2), channel_id=1, source_target_pairs={{0,1},{1,2},{2,3},{3,4},{4,5},{5,6},{6,7},{7,8},{8,9},{9,10},{10,1... | collective-permute-start | bytes 1966088 | tf_op jit(solution)/shard_map/ppermute | solution.py:14
  50.2 7.0 %copy-start.12 = (bf16[128,2560]{1,0:T(8,128)(2,1)}, bf16[128,2560]{1,0:T(8,128)(2,1)S(1)}, u32[]{:S(2)}) copy-start(bf16[128,2560]{1,0:T(8,128)(2,1)S(1)} %collective-permute-done.10) | copy-start | bytes 1966084
  50.2 14.0 %collective-permute-start.11 = (bf16[128,2560]{1,0:T(8,128)(2,1)S(1)}, bf16[128,2560]{1,0:T(8,128)(2,1)S(1)}, u32[]{:S(2)}, u32[]{:S(2)}) collective-permute-start(bf16[128,2560]{1,0:T(8,128)(2,1)S(1)} %collective-permute-done.10), channel_id=1, source_target_pairs={{0,1},{1,2},{2,3},{3,4},{4,5},{5,6},{6,7},{7,8},{8,9},{9,10},{10,1... | collective-permute-start | bytes 1966088 | tf_op jit(solution)/shard_map/ppermute | solution.py:14
  57.2 14.8 %copy-start.20 = (bf16[128,2560]{1,0:T(8,128)(2,1)}, bf16[128,2560]{1,0:T(8,128)(2,1)S(1)}, u32[]{:S(2)}) copy-start(bf16[128,2560]{1,0:T(8,128)(2,1)S(1)} %collective-permute-done.3) | copy-start | bytes 1966084
  57.2 14.8 %collective-permute-start.4 = (bf16[128,2560]{1,0:T(8,128)(2,1)S(1)}, bf16[128,2560]{1,0:T(8,128)(2,1)S(1)}, u32[]{:S(2)}, u32[]{:S(2)}) collective-permute-start(bf16[128,2560]{1,0:T(8,128)(2,1)S(1)} %collective-permute-done.3), channel_id=1, source_target_pairs={{0,1},{1,2},{2,3},{3,4},{4,5},{5,6},{6,7},{7,8},{8,9},{9,10},{10,1... | collective-permute-start | bytes 1966088 | tf_op jit(solution)/shard_map/ppermute | solution.py:14
  64.2 28.9 %copy-start.16 = (bf16[128,2560]{1,0:T(8,128)(2,1)}, bf16[128,2560]{1,0:T(8,128)(2,1)S(1)}, u32[]{:S(2)}) copy-start(bf16[128,2560]{1,0:T(8,128)(2,1)S(1)} %collective-permute-done.11) | copy-start | bytes 1966084
  64.2 17.0 %collective-permute-start.12 = (bf16[128,2560]{1,0:T(8,128)(2,1)S(1)}, bf16[128,2560]{1,0:T(8,128)(2,1)}, u32[]{:S(2)}, u32[]{:S(2)}) collective-permute-start(bf16[128,2560]{1,0:T(8,128)(2,1)S(1)} %collective-permute-done.11), channel_id=1, source_target_pairs={{0,1},{1,2},{2,3},{3,4},{4,5},{5,6},{6,7},{7,8},{8,9},{9,10},{10,1... | collective-permute-start | bytes 1966088 | tf_op jit(solution)/shard_map/ppermute | solution.py:14
  72.0 23.7 %copy-start.22 = (bf16[128,2560]{1,0:T(8,128)(2,1)}, bf16[128,2560]{1,0:T(8,128)(2,1)S(1)}, u32[]{:S(2)}) copy-start(bf16[128,2560]{1,0:T(8,128)(2,1)S(1)} %collective-permute-done.4) | copy-start | bytes 1966084
  72.0 14.0 %collective-permute-start.5 = (bf16[128,2560]{1,0:T(8,128)(2,1)S(1)}, bf16[128,2560]{1,0:T(8,128)(2,1)}, u32[]{:S(2)}, u32[]{:S(2)}) collective-permute-start(bf16[128,2560]{1,0:T(8,128)(2,1)S(1)} %collective-permute-done.4), channel_id=1, source_target_pairs={{0,1},{1,2},{2,3},{3,4},{4,5},{5,6},{6,7},{7,8},{8,9},{9,10},{10,1... | collective-permute-start | bytes 1966088 | tf_op jit(solution)/shard_map/ppermute | solution.py:14
  81.2 16.1 %collective-permute-start.13 = (bf16[128,2560]{1,0:T(8,128)(2,1)}, bf16[128,2560]{1,0:T(8,128)(2,1)}, u32[]{:S(2)}, u32[]{:S(2)}) collective-permute-start(bf16[128,2560]{1,0:T(8,128)(2,1)} %collective-permute-done.12), channel_id=1, source_target_pairs={{0,1},{1,2},{2,3},{3,4},{4,5},{5,6},{6,7},{7,8},{8,9},{9,10},{10,1... | collective-permute-start | bytes 1966088 | tf_op jit(solution)/shard_map/ppermute | solution.py:14
  86.0 18.1 %collective-permute-start.6 = (bf16[128,2560]{1,0:T(8,128)(2,1)}, bf16[128,2560]{1,0:T(8,128)(2,1)}, u32[]{:S(2)}, u32[]{:S(2)}) collective-permute-start(bf16[128,2560]{1,0:T(8,128)(2,1)} %collective-permute-done.5), channel_id=1, source_target_pairs={{0,1},{1,2},{2,3},{3,4},{4,5},{5,6},{6,7},{7,8},{8,9},{9,10},{10,1... | collective-permute-start | bytes 1966088 | tf_op jit(solution)/shard_map/ppermute | solution.py:14
  97.3 13.3 %collective-permute-start.14 = (bf16[128,2560]{1,0:T(8,128)(2,1)}, bf16[128,2560]{1,0:T(8,128)(2,1)}, u32[]{:S(2)}, u32[]{:S(2)}) collective-permute-start(bf16[128,2560]{1,0:T(8,128)(2,1)} %collective-permute-done.13), channel_id=1, source_target_pairs={{0,1},{1,2},{2,3},{3,4},{4,5},{5,6},{6,7},{7,8},{8,9},{9,10},{10,1... | collective-permute-start | bytes 1966088 | tf_op jit(solution)/shard_map/ppermute | solution.py:14
  104.2 14.0 %collective-permute-start.7 = (bf16[128,2560]{1,0:T(8,128)(2,1)}, bf16[128,2560]{1,0:T(8,128)(2,1)S(1)}, u32[]{:S(2)}, u32[]{:S(2)}) collective-permute-start(bf16[128,2560]{1,0:T(8,128)(2,1)} %collective-permute-done.6), channel_id=1, source_target_pairs={{0,1},{1,2},{2,3},{3,4},{4,5},{5,6},{6,7},{7,8},{8,9},{9,10},{10,1... | collective-permute-start | bytes 1966088 | tf_op jit(solution)/shard_map/ppermute | solution.py:14
  110.6 12.6 %copy-start.23 = (bf16[128,2560]{1,0:T(8,128)(2,1)S(1)}, bf16[128,2560]{1,0:T(8,128)(2,1)}, u32[]{:S(2)}) copy-start(bf16[128,2560]{1,0:T(8,128)(2,1)} %copy-done.22) | copy-start | bytes 1966084
  110.6 26.9 %collective-permute-start.15 = (bf16[128,2560]{1,0:T(8,128)(2,1)}, bf16[128,2560]{1,0:T(8,128)(2,1)}, u32[]{:S(2)}, u32[]{:S(2)}) collective-permute-start(bf16[128,2560]{1,0:T(8,128)(2,1)} %collective-permute-done.14), channel_id=1, source_target_pairs={{0,1},{1,2},{2,3},{3,4},{4,5},{5,6},{6,7},{7,8},{8,9},{9,10},{10,1... | collective-permute-start | bytes 1966088 | tf_op jit(solution)/shard_map/ppermute | solution.py:14
  139.6 6.2 %copy-start.17 = (bf16[128,2560]{1,0:T(8,128)(2,1)S(1)}, bf16[128,2560]{1,0:T(8,128)(2,1)}, u32[]{:S(2)}) copy-start(bf16[128,2560]{1,0:T(8,128)(2,1)} %copy-done.16) | copy-start | bytes 1966084
  361.5 47.7 %collective-permute-start.17 = (f32[24,7680]{1,0:T(8,128)}, f32[24,7680]{1,0:T(8,128)}, u32[]{:S(2)}, u32[]{:S(2)}) collective-permute-start(f32[24,7680]{1,0:T(8,128)} %fusion), channel_id=1, source_target_pairs={{0,2},{1,3},{2,4},{3,5},{4,6},{5,7},{6,8},{7,9},{8,10},{9,11},{10,... | collective-permute-start | bytes 2211848
  381.4 28.6 %collective-permute-start.16 = (f32[24,7680]{1,0:T(8,128)}, f32[24,7680]{1,0:T(8,128)}, u32[]{:S(2)}, u32[]{:S(2)}) collective-permute-start(f32[24,7680]{1,0:T(8,128)} %fusion), channel_id=1, source_target_pairs={{0,1},{1,2},{2,3},{3,4},{4,5},{5,6},{6,7},{7,8},{8,9},{9,10},{10,1... | collective-permute-start | bytes 2211848
  388.8 20.4 %collective-permute-start.18 = (f32[12,7680]{1,0:T(8,128)S(1)}, f32[12,7680]{1,0:T(8,128)S(1)}, u32[]{:S(2)}, u32[]{:S(2)}) collective-permute-start(f32[12,7680]{1,0:T(8,128)S(1)} %slice.15), channel_id=1, source_target_pairs={{0,3},{1,4},{2,5},{3,6},{4,7},{5,8},{6,9},{7,10},{8,11},{9,12},{10... | collective-permute-start | bytes 1105928
  402.9 7.1 %copy-start.3 = (f32[24,7680]{1,0:T(8,128)S(1)}, f32[24,7680]{1,0:T(8,128)}, u32[]{:S(2)}) copy-start(f32[24,7680]{1,0:T(8,128)} %fusion) | copy-start | bytes 2211844
  (17 other events, 46.0 us)
Sparse Core Ops, SparseCore 0:
  81.3 73.0 all-gather.2
where the time goes:
time: 504 us; the launch traced here: 502 us
  blocking collectives  213 us (42%)
  starting transfers between devices  139 us (28%)
  local copies, waits for them, and re-layouts  95.2 us (19%)
  matrix products  22.1 us (4%)
  between operations  15.1 us (3%)
  other arithmetic  14.2 us (3%)
    unnamed x1, blocking collectives  139 us
    ppermute x16, starting transfers between devices, from_behind(): lax.ppermute(value, axis, [(source, source + steps) for source in range(f...  103 us
    psum x1, blocking collectives, shards(): lax.psum((jnp.sum(fast_weights * fast_weights, axis=0), jnp.sum(moved * m...  74 us
    unnamed x84, local copies, waits for them, and re-layouts  49.1 us
    unnamed x3, starting transfers between devices  36.1 us
    mul x1, local copies, waits for them, and re-layouts, shards(): jnp.stack([first, third, second], axis=1).reshape(head_width, -1)  11.7 us
  transfers between devices with their start and end apart: 20, of which 1 were waited for; matrix products, arithmetic and copies ran while one was open for 14% of the time, Pallas kernels for 0%

commit v1 on v0

v1 whole, which is shorter than its diff:
```python
import functools
import math

import jax
import jax.numpy as jnp
from jax import lax
from jax.experimental import pallas as pl
from jax.experimental.pallas import tpu as pltpu
from jax.sharding import PartitionSpec as P

WINDOW = 1024
LANES = 128
F32 = jnp.float32
BF16 = jnp.bfloat16


def dot(a, b):
    return jnp.dot(a, b, preferred_element_type=F32)


def dot_nt(a, b):
    return lax.dot_general(a, b, (((1,), (1,)), ((), ())), preferred_element_type=F32)


def dot_tn(a, b):
    return lax.dot_general(a, b, (((0,), (0,)), ((), ())), preferred_element_type=F32)


def kernel(
    n, heads, width,
    q_in, k_in, v_in, step_in, w_in, gains,
    out, g_out, scale_out,
    qb, kb, vb, stb, wb, wfull, kn, hid, tgt, gg, gu,
    gstage, ginc, gsend, sums, sinc, scale_send, ostage,
    s_in, r_q, r_k, r_v, r_st, r_w,
    s_wf, s_kf, s_vf,
    s_gp, r_gp, s_sp, r_sp, s_g, r_g, s_sc, r_sc, s_o, r_o,
):
    group = n // heads
    rows = width // n
    span = heads * LANES
    scale = 1.0 / math.sqrt(width)
    me = lax.axis_index("seq")
    head = me // group
    member = me % group
    block_member = me // heads
    block_slot = me % heads

    def remote(src, dst, send, recv, device):
        return pltpu.make_async_remote_copy(
            src_ref=src, dst_ref=dst, send_sem=send, recv_sem=recv,
            device_id={"seq": device}, device_id_type=pl.DeviceIdType.MESH,
        )

    barrier = pltpu.get_barrier_semaphore()
    for step in range(1, n):
        pl.semaphore_signal(
            barrier, inc=1, device_id={"seq": lax.rem(me + step, n)},
            device_id_type=pl.DeviceIdType.MESH,
        )
    pl.semaphore_wait(barrier, n - 1)

    def lanes(slot):
        return pl.ds(pl.multiple_of(slot * LANES, LANES), LANES)

    def head_rows(which):
        return pl.ds(pl.multiple_of(which * width, 64), width)

    is_self = block_member == member
    pending = []
    maybe = []

    def spread(src_of, dst, recv, kind):
        for step in range(heads):
            which = lax.rem(head + step, heads)
            device = which * group + block_member
            src = src_of(which)
            copy = remote(src, dst, s_in.at[kind, step], recv, device)
            if step == 0:
                @pl.when(is_self)
                def _():
                    pltpu.make_async_copy(src, dst, recv).start()

                @pl.when(jnp.logical_not(is_self))
                def _():
                    copy.start()
                maybe.append(copy)
            else:
                copy.start()
                pending.append(copy)

    for step in range(heads):
        which = lax.rem(head + step, heads)
        device = which * group + member
        if step == 0:
            pltpu.make_async_copy(w_in.at[which], wb.at[me], r_w.at[me]).start()
        else:
            copy = remote(w_in.at[which], wb.at[me], s_in.at[4, step], r_w.at[me], device)
            copy.start()
            pending.append(copy)
    own = heads + block_slot
    spread(lambda w: k_in.at[head_rows(w), :], kb.at[:, lanes(own)], r_k.at[own], 0)
    spread(lambda w: v_in.at[head_rows(w), :], vb.at[:, lanes(own)], r_v.at[own], 1)
    spread(lambda w: step_in, stb.at[block_slot], r_st.at[block_slot], 2)
    spread(lambda w: q_in.at[head_rows(w), :], qb.at[:, lanes(block_slot)], r_q.at[block_slot], 3)

    @pl.when(member == 0)
    def _():
        kb[:, :span] = jnp.zeros((width, span), BF16)
        vb[:, :span] = jnp.zeros((width, span), BF16)

    def landed(ref, sem):
        pltpu.make_async_copy(ref, ref, sem).wait()

    for i in range(heads):
        slot = member + group * i
        landed(wb.at[slot], r_w.at[slot])
        for d in range(1, group):
            copy = remote(
                wb.at[slot], wb.at[slot], s_wf.at[i, d - 1], r_w.at[slot],
                head * group + lax.rem(member + d, group),
            )
            copy.start()
            pending.append(copy)

    forwards = []
    for i in range(heads):
        a, b = (heads + i) * LANES, i * LANES
        for buf, send, recv in ((kb, s_kf, r_k), (vb, s_vf, r_v)):
            landed(buf.at[:, pl.ds(a, LANES)], recv.at[heads + i])
            copy = remote(
                buf.at[:, pl.ds(a, LANES)], buf.at[:, pl.ds(b, LANES)], send.at[i], recv.at[i], me + 1
            )
            forwards.append(copy)

            @pl.when(member < group - 1)
            def _():
                copy.start()
    for d in range(1, group):
        for i in range(heads):
            slot = lax.rem(member + d, group) + group * i
            landed(wb.at[slot], r_w.at[slot])
    for s in range(n):
        piece = wb[s].astype(F32)
        for m in range(3):
            wfull[m, s * rows : (s + 1) * rows, :] = piece[m * rows : (m + 1) * rows, :]
    for i in range(heads):
        landed(stb.at[i], r_st.at[i])

    w1 = wfull[0].astype(BF16)
    w3 = wfull[1].astype(BF16)
    w2 = wfull[2].astype(BF16)

    for i in range(heads):
        here = pl.ds(span + i * LANES, LANES)
        there = pl.ds(i * LANES, LANES)
        tgt[:, there] = (-stb[i, pl.ds(head, 1), :] * vb[:, here].astype(F32)).astype(BF16)
    chunk = 2 * LANES

    def grad_chunk(c, carry):
        here = pl.ds(pl.multiple_of(span + c * chunk, chunk), chunk)
        there = pl.ds(pl.multiple_of(c * chunk, chunk), chunk)
        keys = kb[:, here]
        gate = dot_tn(w1, keys) * scale
        up = dot_tn(w3, keys) * scale
        back = dot(w2, tgt[:, there]) * scale
        sigma = jax.nn.sigmoid(gate)
        silu = gate * sigma
        hid[:, there] = (silu * up).astype(BF16)
        gg[:, there] = (back * up * (sigma * (1.0 + gate * (1.0 - sigma)))).astype(BF16)
        gu[:, there] = (back * silu).astype(BF16)
        return carry

    lax.fori_loop(0, span // chunk, grad_chunk, 0)
    own_keys = kb[:, span:]
    for m, (left, right) in enumerate(((own_keys, gg), (own_keys, gu), (hid[...], tgt))):
        grad = dot_nt(left, right[...]) * scale
        for s in range(n):
            gstage[s % group, s // group, m * rows : (m + 1) * rows, :] = grad[s * rows : (s + 1) * rows, :]

    for d in range(1, group):
        other = lax.rem(member + d, group)
        copy = remote(
            gstage.at[other], ginc.at[d - 1], s_gp.at[d - 1], r_gp.at[d - 1], head * group + other
        )
        copy.start()
        pending.append(copy)

    @pl.when(member > 0)
    def _():
        for i in range(heads):
            landed(kb.at[:, pl.ds(i * LANES, LANES)], r_k.at[i])
            landed(vb.at[:, pl.ds(i * LANES, LANES)], r_v.at[i])

    def flip(c, carry):
        at = pl.ds(pl.multiple_of(c * LANES, LANES), LANES)
        kn[at, :] = kb[:, at].T
        return carry

    lax.fori_loop(0, 2 * heads, flip, 0)

    for d in range(1, group):
        landed(ginc.at[d - 1], r_gp.at[d - 1])
    sums[...] = jnp.zeros_like(sums)

    def add_up(i, carry):
        total = gstage[member, i]
        for d in range(1, group):
            total = total + ginc[d - 1, i]
        gsend[i] = total.astype(BF16)
        weight = wb[member + group * i].astype(F32)
        moved = weight - total
        for m in range(3):
            part = slice(m * rows, (m + 1) * rows)
            old = weight[part, :]
            new = moved[part, :]
            sums[m : m + 1, :] += jnp.sum(old * old, axis=0, keepdims=True)
            sums[4 + m : 5 + m, :] += jnp.sum(new * new, axis=0, keepdims=True)
        return carry

    lax.fori_loop(0, heads, add_up, 0)
    for d in range(1, group):
        copy = remote(
            sums, sinc.at[d - 1], s_sp.at[d - 1], r_sp.at[d - 1],
            head * group + lax.rem(member + d, group),
        )
        copy.start()
        pending.append(copy)

    for i in range(heads):
        landed(qb.at[:, pl.ds(i * LANES, LANES)], r_q.at[i])

    reach = WINDOW + chunk
    key_at = lax.broadcasted_iota(jnp.int32, (reach, chunk), 0)
    query_at = lax.broadcasted_iota(jnp.int32, (reach, chunk), 1)
    distance = WINDOW + query_at - key_at
    in_window = (distance >= 0) & (distance < WINDOW)
    first_key = jnp.where(member == 0, span, 0)

    def normalize(field, gain):
        mean_sq = jnp.mean(field * field, axis=0, keepdims=True)
        return field * lax.rsqrt(mean_sq + 1e-05) * gain

    outs = []

    def attend(c):
        start = c * chunk
        query = qb[:, pl.ds(start, chunk)]
        scores = dot(kn[pl.ds(start, reach), :], query) * scale
        allowed = in_window & (key_at + start >= first_key)
        scores = jnp.where(allowed, scores, -1e30)
        weights = jnp.exp(scores - jnp.max(scores, axis=0, keepdims=True))
        probs = (weights / jnp.sum(weights, axis=0, keepdims=True)).astype(BF16)
        attended = dot(vb[:, pl.ds(start, reach)], probs)
        window_part = normalize(attended, gains[1, :, 0:1])
        gate = dot_tn(w1, query) * scale
        up = dot_tn(w3, query) * scale
        hidden = (gate * jax.nn.sigmoid(gate) * up).astype(BF16)
        fast_part = normalize(dot_tn(w2, hidden) * scale, gains[0, :, 0:1])
        result = (fast_part + window_part).astype(BF16)
        for half in range(2):
            i = 2 * c + half
            ostage[i] = result[:, half * LANES : (half + 1) * LANES]
            device = member * heads + i
            dst = out.at[head_rows(head), :]
            copy = remote(ostage.at[i], dst, s_o.at[i], r_o.at[head], device)
            outs.append((copy, device))

            @pl.when(device == me)
            def _():
                pltpu.make_async_copy(ostage.at[i], dst, r_o.at[head]).start()

            @pl.when(device != me)
            def _():
                copy.start()

    attend(0)
    for d in range(1, group):
        landed(sinc.at[d - 1], r_sp.at[d - 1])
    total = sums[...]
    for d in range(1, group):
        total = total + sinc[d - 1]
    scale_send[0:4, :] = jnp.sqrt((total[0:4] + 1e-06) / (total[4:8] + 1e-06))
    scale_send[4:8, :] = total[4:8]
    for step in range(heads):
        i = lax.rem(head + step, heads)
        device = member + group * i
        if step == 0:
            pltpu.make_async_copy(gsend.at[i], g_out.at[head], r_g.at[head]).start()
            pltpu.make_async_copy(scale_send, scale_out.at[head], r_sc.at[head]).start()
        else:
            copy = remote(gsend.at[i], g_out.at[head], s_g.at[step], r_g.at[head], device)
            copy.start()
            pending.append(copy)
            copy = remote(scale_send, scale_out.at[head], s_sc.at[step], r_sc.at[head], device)
            copy.start()
            pending.append(copy)
    for c in range(1, span // chunk):
        attend(c)

    for i in range(heads):
        landed(g_out.at[i], r_g.at[i])
        landed(scale_out.at[i], r_sc.at[i])
        landed(out.at[pl.ds(i * width, width), :], r_o.at[i])
    for copy in pending:
        copy.wait_send()

    @pl.when(jnp.logical_not(is_self))
    def _():
        for copy in maybe:
            copy.wait_send()

    @pl.when(member < group - 1)
    def _():
        for copy in forwards:
            copy.wait_send()
    for copy, device in outs:
        @pl.when(device != me)
        def _():
            copy.wait_send()


def shards(queries, key_vectors, value_vectors, step_sizes, fast_weights, fast_gain, window_gain):
    tokens = queries.shape[0]
    heads = step_sizes.shape[1]
    width = queries.shape[1] // heads
    n = lax.axis_size("seq")
    group = n // heads
    rows = width // n
    assert tokens == LANES and heads * tokens == WINDOW
    head = lax.axis_index("seq") // group
    q_t, k_t, v_t = queries.T, key_vectors.T, value_vectors.T
    pieces = (
        fast_weights.astype(BF16).reshape(rows, 3, heads, width).transpose(2, 1, 0, 3)
        .reshape(heads, 3 * rows, width)
    )
    gains = jnp.stack([fast_gain.reshape(heads, width), window_gain.reshape(heads, width)], axis=1)
    gains = lax.dynamic_index_in_dim(gains, head, 0, keepdims=False)
    gains = jnp.broadcast_to(gains[:, :, None], (2, width, LANES))
    span = heads * LANES
    vmem = pl.BlockSpec(memory_space=pltpu.VMEM)
    dma = pltpu.SemaphoreType.DMA
    more = max(group - 1, 1)
    out_t, grads, scales = pl.pallas_call(
        functools.partial(kernel, n, heads, width),
        out_shape=(
            jax.ShapeDtypeStruct((heads * width, LANES), BF16),
            jax.ShapeDtypeStruct((heads, 3 * rows, width), BF16),
            jax.ShapeDtypeStruct((heads, 8, width), F32),
        ),
        in_specs=[vmem] * 6,
        out_specs=(vmem, vmem, vmem),
        scratch_shapes=[
            pltpu.VMEM((width, span), BF16),
            pltpu.VMEM((width, 2 * span), BF16),
            pltpu.VMEM((width, 2 * span), BF16),
            pltpu.VMEM((heads, heads, LANES), F32),
            pltpu.VMEM((n, 3 * rows, width), BF16),
            pltpu.VMEM((3, width, width), F32),
            pltpu.VMEM((2 * span, width), BF16),
            pltpu.VMEM((width, span), BF16),
            pltpu.VMEM((width, span), BF16),
            pltpu.VMEM((width, span), BF16),
            pltpu.VMEM((width, span), BF16),
            pltpu.VMEM((group, heads, 3 * rows, width), F32),
            pltpu.VMEM((more, heads, 3 * rows, width), F32),
            pltpu.VMEM((heads, 3 * rows, width), BF16),
            pltpu.VMEM((8, width), F32),
            pltpu.VMEM((more, 8, width), F32),
            pltpu.VMEM((8, width), F32),
            pltpu.VMEM((heads, width, LANES), BF16),
            dma((5, heads)), dma((heads,)), dma((2 * heads,)), dma((2 * heads,)), dma((heads,)), dma((n,)),
            dma((heads, more)), dma((heads,)), dma((heads,)),
            dma((more,)), dma((more,)), dma((more,)), dma((more,)),
            dma((heads,)), dma((heads,)), dma((heads,)), dma((heads,)), dma((heads,)), dma((heads,)),
        ],
        compiler_params=pltpu.CompilerParams(
            collective_id=0, has_side_effects=True, vmem_limit_bytes=60 << 20
        ),
        name="ttt",
    )(q_t, k_t, v_t, step_sizes.T, pieces, gains)
    layer_out = out_t.T
    momentum = (
        grads.astype(F32).reshape(heads, 3, rows, width).transpose(2, 1, 0, 3).reshape(rows, 3 * heads * width)
    )
    column_scale = scales[:, :3, :].transpose(1, 0, 2).reshape(1, -1)
    new_weights = (fast_weights - momentum) * column_scale
    return (layer_out, new_weights, momentum)


def solution(mesh):
    in_specs = (
        P(("groups", "seq"), None),
        P(("groups", "seq"), None),
        P(("groups", "seq"), None),
        P(("groups", "seq"), None),
        P("seq", None),
        P(),
        P(),
    )
    out_specs = (P(("groups", "seq"), None), P(("groups", "seq"), None), P(("groups", "seq"), None))
    return jax.shard_map(shards, mesh=mesh, in_specs=in_specs, out_specs=out_specs, check_vma=False)
```

time: 504 us -> 104 us (0.21)
  the two profiles are of different devices: /device:TPU:0 before, /device:TPU:13 now
where the time goes in v1:
time: 104 us
  Pallas kernels  89.8 us (86%)
  local copies, waits for them, and re-layouts  10.9 us (10%)
  other arithmetic  2.2 us (2%)
    pallas_call x1, Pallas kernels, shards(): pl.pallas_call(functools.partial(kernel, n, heads, width), out_shape=(jax...  89.8 us
    unnamed x22, local copies, waits for them, and re-layouts  8.15 us

profile of v1, /device:TPU:13, one launch (start us, length us, event | category | flops | bytes accessed | tf_op | source)
XLA Modules:
  0.0 103.7 jit_solution(14706261154322427062)
XLA Ops:
  0.6 0.0 copy-start.7
  0.7 0.7 copy-done.7
  1.3 0.0 copy-start.8
  1.3 0.1 stack_reshape.6
  1.4 0.6 copy-done.8
  2.0 0.1 stack_reshape.7
  2.1 0.9 broadcast_in_dim.9.gains
  3.0 1.2 %convert_element_type.4 = bf16[20,7680]{1,0:T(8,128)(2,1)S(1)} convert(f32[20,7680]{1,0:T(8,128)} %param.11) | non-fusion elementwise | flops 153600 | bytes 921600 | tf_op jit(solution)/shard_map/convert_element_type | solution.py:334
  4.2 0.3 reshape.26
  4.5 0.0 copy-start.2
  4.5 0.8 copy.27.w_in
  5.3 0.4 copy-done.2
  5.7 0.0 copy-start.3
  5.7 1.1 %copy.23 = bf16[128,2560]{0,1:T(8,128)(2,1)} copy(bf16[128,2560]{1,0:T(8,128)(2,1)S(1)} %copy-done.2) | data formatting | bytes 1310720 | tf_op args[0]
  6.8 0.0 copy-done.3
  6.8 0.0 copy-start.4
  6.8 1.1 %copy.24 = bf16[128,2560]{0,1:T(8,128)(2,1)} copy(bf16[128,2560]{1,0:T(8,128)(2,1)S(1)} %copy-done.3) | data formatting | bytes 1310720 | tf_op args[1]
  7.9 0.0 copy-done.4
  7.9 1.1 %copy.25 = bf16[128,2560]{0,1:T(8,128)(2,1)} copy(bf16[128,2560]{1,0:T(8,128)(2,1)S(1)} %copy-done.4) | data formatting | bytes 1310720 | tf_op args[2]
  9.0 89.8 %ttt.1 = (bf16[2560,128]{1,0:T(8,128)(2,1)}, bf16[8,60,320]{2,1,0:T(8,128)(2,1)}, f32[8,8,320]{2,1,0:T(8,128)}) custom-call(bf16[2560,128]{1,0:T(8,128)(2,1)} %bitcast.17, bf16[2560,128]{1,0:T(8,128)(2,1)} %bitcast.18, bf16[2560,128]{1,0:T(8,128)(2,1)} %bitcast.19, f32[8,128]{1,0:T(8,128)} %bitcast.23, bf16[8,60,320]{2,1,0:T(8,128)(2,1)} %copy.27.w_in, ...), custom_call_target="tpu_custom_call" | custom-call | tf_op jit(solution)/shard_map/ttt/pallas_call | solution.py:344
  98.8 0.0 copy-start.6
  98.8 0.0 copy-start.5
  98.8 2.2 %copy.31 = bf16[128,2560]{1,0:T(8,128)(2,1)} copy(bf16[128,2560]{0,1:T(8,128)(2,1)} %bitcast.22) | data formatting | bytes 1310720
  101.1 0.0 copy-done.6
  101.1 0.1 mul.10
  101.2 0.0 copy-done.5
  101.2 0.2 copy.28
  101.5 0.0 copy-start
  101.5 0.2 reshape.32
  101.7 0.9 copy-done
  102.6 1.0 subtract_multiply_fusion
  103.6 0.1 copy-done.1
  (6 shorter events, 0.1 us)
Async XLA Ops:
  0.6 0.7 copy-start.7
  1.3 0.7 copy-start.8
  4.5 1.2 %copy-start.2 = (bf16[128,2560]{1,0:T(8,128)(2,1)S(1)}, bf16[128,2560]{1,0:T(8,128)(2,1)}, u32[]{:S(2)}) copy-start(bf16[128,2560]{1,0:T(8,128)(2,1)} %param.7) | copy-start | bytes 1966084
  5.7 1.1 %copy-start.3 = (bf16[128,2560]{1,0:T(8,128)(2,1)S(1)}, bf16[128,2560]{1,0:T(8,128)(2,1)}, u32[]{:S(2)}) copy-start(bf16[128,2560]{1,0:T(8,128)(2,1)} %param.8) | copy-start | bytes 1966084
  6.8 1.1 %copy-start.4 = (bf16[128,2560]{1,0:T(8,128)(2,1)S(1)}, bf16[128,2560]{1,0:T(8,128)(2,1)}, u32[]{:S(2)}) copy-start(bf16[128,2560]{1,0:T(8,128)(2,1)} %param.9) | copy-start | bytes 1966084
  98.8 2.2 %copy-start.6 = (f32[8,8,320]{2,1,0:T(8,128)S(1)}, f32[8,8,320]{2,1,0:T(8,128)}, u32[]{:S(2)}) copy-start(f32[8,8,320]{2,1,0:T(8,128)} %get-tuple-element.8) | copy-start | bytes 245764
  98.8 2.3 %copy-start.5 = (bf16[8,60,320]{2,1,0:T(8,128)(2,1)S(1)}, bf16[8,60,320]{2,1,0:T(8,128)(2,1)}, u32[]{:S(2)}) copy-start(bf16[8,60,320]{2,1,0:T(8,128)(2,1)} %get-tuple-element.7) | copy-start | bytes 921604
  101.5 1.1 %copy-start = (f32[20,7680]{1,0:T(8,128)S(1)}, f32[20,7680]{1,0:T(8,128)}, u32[]{:S(2)}) copy-start(f32[20,7680]{1,0:T(8,128)} %param.11) | copy-start | bytes 1843204
  102.6 1.1 %copy-start.1 = (f32[20,7680]{1,0:T(8,128)}, f32[20,7680]{1,0:T(8,128)S(1)}, u32[]{:S(2)}) copy-start(f32[20,7680]{1,0:T(8,128)S(1)} %reshape.32) | copy-start | bytes 1843204

commit v2 on v1

--- a/solution.py
+++ b/solution.py
@@ -27,7 +27,7 @@
 
 
 def kernel(
-    n, heads, width,
+    n, groups, heads, width,
     q_in, k_in, v_in, step_in, w_in, gains,
     out, g_out, scale_out,
     qb, kb, vb, stb, wb, wfull, kn, hid, tgt, gg, gu,
@@ -41,15 +41,17 @@
     span = heads * LANES
     scale = 1.0 / math.sqrt(width)
     me = lax.axis_index("seq")
+    part = lax.axis_index("groups")
     head = me // group
     member = me % group
     block_member = me // heads
     block_slot = me % heads
 
-    def remote(src, dst, send, recv, device):
+    def remote(src, dst, send, recv, device, to_part=None):
         return pltpu.make_async_remote_copy(
             src_ref=src, dst_ref=dst, send_sem=send, recv_sem=recv,
-            device_id={"seq": device}, device_id_type=pl.DeviceIdType.MESH,
+            device_id={"groups": part if to_part is None else to_part, "seq": device},
+            device_id_type=pl.DeviceIdType.MESH,
         )
 
     barrier = pltpu.get_barrier_semaphore()
@@ -58,10 +60,14 @@
             barrier, inc=1, device_id={"seq": lax.rem(me + step, n)},
             device_id_type=pl.DeviceIdType.MESH,
         )
-    pl.semaphore_wait(barrier, n - 1)
-
-    def lanes(slot):
-        return pl.ds(pl.multiple_of(slot * LANES, LANES), LANES)
+    for other in range(1, groups):
+        for d in range(group):
+            pl.semaphore_signal(
+                barrier, inc=1,
+                device_id={"groups": lax.rem(part + other, groups), "seq": head * group + d},
+                device_id_type=pl.DeviceIdType.MESH,
+            )
+    pl.semaphore_wait(barrier, n - 1 + (groups - 1) * group)
 
     def head_rows(which):
         return pl.ds(pl.multiple_of(which * width, 64), width)
@@ -89,57 +95,71 @@
                 copy.start()
                 pending.append(copy)
 
-    for step in range(heads):
-        which = lax.rem(head + step, heads)
-        device = which * group + member
+    stride = heads // groups
+    shift = lax.rem(part + groups * heads - 2 * head, groups)
+    w_maybe = []
+    for step in range(stride):
+        offset = shift + groups * step
+        which = lax.rem(head + offset, heads)
+        copy = remote(w_in.at[which], wb.at[me], s_in.at[4, step], r_w.at[me], which * group + member)
         if step == 0:
-            pltpu.make_async_copy(w_in.at[which], wb.at[me], r_w.at[me]).start()
+            @pl.when(offset == 0)
+            def _():
+                pltpu.make_async_copy(w_in.at[which], wb.at[me], r_w.at[me]).start()
+
+            @pl.when(offset != 0)
+            def _():
+                copy.start()
+            w_maybe.append(copy)
         else:
-            copy = remote(w_in.at[which], wb.at[me], s_in.at[4, step], r_w.at[me], device)
             copy.start()
             pending.append(copy)
     own = heads + block_slot
-    spread(lambda w: k_in.at[head_rows(w), :], kb.at[:, lanes(own)], r_k.at[own], 0)
-    spread(lambda w: v_in.at[head_rows(w), :], vb.at[:, lanes(own)], r_v.at[own], 1)
+    spread(lambda w: k_in.at[head_rows(w), :], kb.at[own], r_k.at[own], 0)
+    spread(lambda w: v_in.at[head_rows(w), :], vb.at[own], r_v.at[own], 1)
     spread(lambda w: step_in, stb.at[block_slot], r_st.at[block_slot], 2)
-    spread(lambda w: q_in.at[head_rows(w), :], qb.at[:, lanes(block_slot)], r_q.at[block_slot], 3)
+    spread(lambda w: q_in.at[head_rows(w), :], qb.at[block_slot], r_q.at[block_slot], 3)
 
     @pl.when(member == 0)
     def _():
-        kb[:, :span] = jnp.zeros((width, span), BF16)
-        vb[:, :span] = jnp.zeros((width, span), BF16)
+        kb[:heads] = jnp.zeros((heads, width, LANES), BF16)
+        vb[:heads] = jnp.zeros((heads, width, LANES), BF16)
 
     def landed(ref, sem):
         pltpu.make_async_copy(ref, ref, sem).wait()
 
-    for i in range(heads):
-        slot = member + group * i
+    first = lax.rem(part + groups * heads - head, groups)
+    for t in range(stride):
+        slot = member + group * (first + groups * t)
         landed(wb.at[slot], r_w.at[slot])
-        for d in range(1, group):
-            copy = remote(
-                wb.at[slot], wb.at[slot], s_wf.at[i, d - 1], r_w.at[slot],
-                head * group + lax.rem(member + d, group),
-            )
-            copy.start()
-            pending.append(copy)
+        for other in range(groups):
+            for d in range(group):
+                if other + d == 0:
+                    continue
+                copy = remote(
+                    wb.at[slot], wb.at[slot], s_wf.at[t, other * group + d], r_w.at[slot],
+                    head * group + lax.rem(member + d, group), lax.rem(part + other, groups),
+                )
+                copy.start()
+                pending.append(copy)
 
     forwards = []
     for i in range(heads):
-        a, b = (heads + i) * LANES, i * LANES
         for buf, send, recv in ((kb, s_kf, r_k), (vb, s_vf, r_v)):
-            landed(buf.at[:, pl.ds(a, LANES)], recv.at[heads + i])
-            copy = remote(
-                buf.at[:, pl.ds(a, LANES)], buf.at[:, pl.ds(b, LANES)], send.at[i], recv.at[i], me + 1
-            )
+            landed(buf.at[heads + i], recv.at[heads + i])
+            copy = remote(buf.at[heads + i], buf.at[i], send.at[i], recv.at[i], me + 1)
             forwards.append(copy)
 
             @pl.when(member < group - 1)
             def _():
                 copy.start()
-    for d in range(1, group):
-        for i in range(heads):
-            slot = lax.rem(member + d, group) + group * i
-            landed(wb.at[slot], r_w.at[slot])
+    for d in range(group):
+        for e in range(groups):
+            if d + e == 0:
+                continue
+            for t in range(stride):
+                slot = lax.rem(member + d, group) + group * (lax.rem(first + e, groups) + groups * t)
+                landed(wb.at[slot], r_w.at[slot])
     for s in range(n):
         piece = wb[s].astype(F32)
         for m in range(3):
@@ -152,15 +172,13 @@
     w2 = wfull[2].astype(BF16)
 
     for i in range(heads):
-        here = pl.ds(span + i * LANES, LANES)
         there = pl.ds(i * LANES, LANES)
-        tgt[:, there] = (-stb[i, pl.ds(head, 1), :] * vb[:, here].astype(F32)).astype(BF16)
+        tgt[:, there] = (-stb[i, pl.ds(head, 1), :] * vb[heads + i].astype(F32)).astype(BF16)
     chunk = 2 * LANES
 
     def grad_chunk(c, carry):
-        here = pl.ds(pl.multiple_of(span + c * chunk, chunk), chunk)
         there = pl.ds(pl.multiple_of(c * chunk, chunk), chunk)
-        keys = kb[:, here]
+        keys = jnp.concatenate([kb[heads + 2 * c], kb[heads + 2 * c + 1]], axis=1)
         gate = dot_tn(w1, keys) * scale
         up = dot_tn(w3, keys) * scale
         back = dot(w2, tgt[:, there]) * scale
@@ -172,7 +190,7 @@
         return carry
 
     lax.fori_loop(0, span // chunk, grad_chunk, 0)
-    own_keys = kb[:, span:]
+    own_keys = jnp.concatenate([kb[heads + i] for i in range(heads)], axis=1)
     for m, (left, right) in enumerate(((own_keys, gg), (own_keys, gu), (hid[...], tgt))):
         grad = dot_nt(left, right[...]) * scale
         for s in range(n):
@@ -189,12 +207,12 @@
     @pl.when(member > 0)
     def _():
         for i in range(heads):
-            landed(kb.at[:, pl.ds(i * LANES, LANES)], r_k.at[i])
-            landed(vb.at[:, pl.ds(i * LANES, LANES)], r_v.at[i])
+            landed(kb.at[i], r_k.at[i])
+            landed(vb.at[i], r_v.at[i])
 
     def flip(c, carry):
         at = pl.ds(pl.multiple_of(c * LANES, LANES), LANES)
-        kn[at, :] = kb[:, at].T
+        kn[at, :] = kb[c].T
         return carry
 
     lax.fori_loop(0, 2 * heads, flip, 0)
@@ -228,7 +246,7 @@
         pending.append(copy)
 
     for i in range(heads):
-        landed(qb.at[:, pl.ds(i * LANES, LANES)], r_q.at[i])
+        landed(qb.at[i], r_q.at[i])
 
     reach = WINDOW + chunk
     key_at = lax.broadcasted_iota(jnp.int32, (reach, chunk), 0)
@@ -245,13 +263,14 @@
 
     def attend(c):
         start = c * chunk
-        query = qb[:, pl.ds(start, chunk)]
+        query = jnp.concatenate([qb[2 * c], qb[2 * c + 1]], axis=1)
         scores = dot(kn[pl.ds(start, reach), :], query) * scale
         allowed = in_window & (key_at + start >= first_key)
         scores = jnp.where(allowed, scores, -1e30)
         weights = jnp.exp(scores - jnp.max(scores, axis=0, keepdims=True))
         probs = (weights / jnp.sum(weights, axis=0, keepdims=True)).astype(BF16)
-        attended = dot(vb[:, pl.ds(start, reach)], probs)
+        values = jnp.concatenate([vb[2 * c + i] for i in range(reach // LANES)], axis=1)
+        attended = dot(values, probs)
         window_part = normalize(attended, gains[1, :, 0:1])
         gate = dot_tn(w1, query) * scale
         up = dot_tn(w3, query) * scale
@@ -310,6 +329,11 @@
         for copy in maybe:
             copy.wait_send()
 
+    @pl.when(shift != 0)
+    def _():
+        for copy in w_maybe:
+            copy.wait_send()
+
     @pl.when(member < group - 1)
     def _():
         for copy in forwards:
@@ -325,6 +349,7 @@
     heads = step_sizes.shape[1]
     width = queries.shape[1] // heads
     n = lax.axis_size("seq")
+    groups = lax.axis_size("groups")
     group = n // heads
     rows = width // n
     assert tokens == LANES and heads * tokens == WINDOW
@@ -342,7 +367,7 @@
     dma = pltpu.SemaphoreType.DMA
     more = max(group - 1, 1)
     out_t, grads, scales = pl.pallas_call(
-        functools.partial(kernel, n, heads, width),
+        functools.partial(kernel, n, groups, heads, width),
         out_shape=(
             jax.ShapeDtypeStruct((heads * width, LANES), BF16),
             jax.ShapeDtypeStruct((heads, 3 * rows, width), BF16),
@@ -351,9 +376,9 @@
         in_specs=[vmem] * 6,
         out_specs=(vmem, vmem, vmem),
         scratch_shapes=[
-            pltpu.VMEM((width, span), BF16),
-            pltpu.VMEM((width, 2 * span), BF16),
-            pltpu.VMEM((width, 2 * span), BF16),
+            pltpu.VMEM((heads, width, LANES), BF16),
+            pltpu.VMEM((2 * heads, width, LANES), BF16),
+            pltpu.VMEM((2 * heads, width, LANES), BF16),
             pltpu.VMEM((heads, heads, LANES), F32),
             pltpu.VMEM((n, 3 * rows, width), BF16),
             pltpu.VMEM((3, width, width), F32),
@@ -370,7 +395,7 @@
             pltpu.VMEM((8, width), F32),
             pltpu.VMEM((heads, width, LANES), BF16),
             dma((5, heads)), dma((heads,)), dma((2 * heads,)), dma((2 * heads,)), dma((heads,)), dma((n,)),
-            dma((heads, more)), dma((heads,)), dma((heads,)),
+            dma((heads // groups, groups * group)), dma((heads,)), dma((heads,)),
             dma((more,)), dma((more,)), dma((more,)), dma((more,)),
             dma((heads,)), dma((heads,)), dma((heads,)), dma((heads,)), dma((heads,)), dma((heads,)),
         ],

time: 104 us -> 99.9 us (0.961)
  Pallas kernels: 89.8 us -> 85.6 us
    pallas_call x1, Pallas kernels: 89.8 us -> 85.6 us  [shards(): pl.pallas_call(functools.partial(kernel, n, groups, heads, width), out_sh...]
where the time goes in v2:
time: 99.9 us; the launch traced here: 99.5 us
  Pallas kernels  85.6 us (86%)
  local copies, waits for them, and re-layouts  10.9 us (11%)
  other arithmetic  2.2 us (2%)
    pallas_call x1, Pallas kernels, shards(): pl.pallas_call(functools.partial(kernel, n, groups, heads, width), out_sh...  85.6 us
    unnamed x22, local copies, waits for them, and re-layouts  8.15 us

profile of v2, /device:TPU:13, one launch (start us, length us, event | category | flops | bytes accessed | tf_op | source)
XLA Modules:
  0.0 99.5 jit_solution(11573527015437022547)
XLA Ops:
  0.6 0.0 copy-start.7
  0.7 0.7 copy-done.7
  1.3 0.0 copy-start.8
  1.3 0.1 stack_reshape.6
  1.4 0.6 copy-done.8
  2.0 0.1 stack_reshape.7
  2.1 0.9 broadcast_in_dim.9.gains
  3.0 1.2 %convert_element_type.4 = bf16[20,7680]{1,0:T(8,128)(2,1)S(1)} convert(f32[20,7680]{1,0:T(8,128)} %param.11) | non-fusion elementwise | flops 153600 | bytes 921600 | tf_op jit(solution)/shard_map/convert_element_type | solution.py:359
  4.2 0.3 reshape.26
  4.5 0.0 copy-start.2
  4.5 0.8 copy.27.w_in
  5.3 0.4 copy-done.2
  5.7 0.0 copy-start.3
  5.7 1.1 %copy.23 = bf16[128,2560]{0,1:T(8,128)(2,1)} copy(bf16[128,2560]{1,0:T(8,128)(2,1)S(1)} %copy-done.2) | data formatting | bytes 1310720 | tf_op args[0]
  6.8 0.0 copy-done.3
  6.8 0.0 copy-start.4
  6.8 1.1 %copy.24 = bf16[128,2560]{0,1:T(8,128)(2,1)} copy(bf16[128,2560]{1,0:T(8,128)(2,1)S(1)} %copy-done.3) | data formatting | bytes 1310720 | tf_op args[1]
  7.9 0.0 copy-done.4
  7.9 1.1 %copy.25 = bf16[128,2560]{0,1:T(8,128)(2,1)} copy(bf16[128,2560]{1,0:T(8,128)(2,1)S(1)} %copy-done.4) | data formatting | bytes 1310720 | tf_op args[2]
  9.0 85.6 %ttt.1 = (bf16[2560,128]{1,0:T(8,128)(2,1)}, bf16[8,60,320]{2,1,0:T(8,128)(2,1)}, f32[8,8,320]{2,1,0:T(8,128)}) custom-call(bf16[2560,128]{1,0:T(8,128)(2,1)} %bitcast.17, bf16[2560,128]{1,0:T(8,128)(2,1)} %bitcast.18, bf16[2560,128]{1,0:T(8,128)(2,1)} %bitcast.19, f32[8,128]{1,0:T(8,128)} %bitcast.23, bf16[8,60,320]{2,1,0:T(8,128)(2,1)} %copy.27.w_in, ...), custom_call_target="tpu_custom_call" | custom-call | tf_op jit(solution)/shard_map/ttt/pallas_call | solution.py:369
  94.6 0.0 copy-start.6
  94.6 0.0 copy-start.5
  94.6 2.2 %copy.31 = bf16[128,2560]{1,0:T(8,128)(2,1)} copy(bf16[128,2560]{0,1:T(8,128)(2,1)} %bitcast.22) | data formatting | bytes 1310720
  96.8 0.0 copy-done.6
  96.8 0.1 mul.10
  96.9 0.0 copy-done.5
  96.9 0.2 copy.28
  97.2 0.0 copy-start
  97.2 0.2 reshape.32
  97.4 0.9 copy-done
  98.3 1.0 %subtract_multiply_fusion = f32[20,7680]{1,0:T(8,128)} fusion(f32[20,7680]{1,0:T(8,128)S(1)} %copy-done, f32[20,7680]{1,0:T(8,128)S(1)} %reshape.32, f32[7680]{0:T(1024)S(1)} %mul.10), kind=kLoop, calls=%fused_computation | loop fusion | flops 307200 | bytes 1873920 | tf_op jit(solution)/shard_map/mul | solution.py:412
  99.4 0.1 copy-done.1
  (6 shorter events, 0.1 us)
Async XLA Ops:
  0.6 0.7 copy-start.7
  1.3 0.7 copy-start.8
  4.5 1.2 %copy-start.2 = (bf16[128,2560]{1,0:T(8,128)(2,1)S(1)}, bf16[128,2560]{1,0:T(8,128)(2,1)}, u32[]{:S(2)}) copy-start(bf16[128,2560]{1,0:T(8,128)(2,1)} %param.7) | copy-start | bytes 1966084
  5.7 1.1 %copy-start.3 = (bf16[128,2560]{1,0:T(8,128)(2,1)S(1)}, bf16[128,2560]{1,0:T(8,128)(2,1)}, u32[]{:S(2)}) copy-start(bf16[128,2560]{1,0:T(8,128)(2,1)} %param.8) | copy-start | bytes 1966084
  6.8 1.1 %copy-start.4 = (bf16[128,2560]{1,0:T(8,128)(2,1)S(1)}, bf16[128,2560]{1,0:T(8,128)(2,1)}, u32[]{:S(2)}) copy-start(bf16[128,2560]{1,0:T(8,128)(2,1)} %param.9) | copy-start | bytes 1966084
  94.6 2.2 %copy-start.6 = (f32[8,8,320]{2,1,0:T(8,128)S(1)}, f32[8,8,320]{2,1,0:T(8,128)}, u32[]{:S(2)}) copy-start(f32[8,8,320]{2,1,0:T(8,128)} %get-tuple-element.8) | copy-start | bytes 245764
  94.6 2.3 %copy-start.5 = (bf16[8,60,320]{2,1,0:T(8,128)(2,1)S(1)}, bf16[8,60,320]{2,1,0:T(8,128)(2,1)}, u32[]{:S(2)}) copy-start(bf16[8,60,320]{2,1,0:T(8,128)(2,1)} %get-tuple-element.7) | copy-start | bytes 921604
  97.2 1.1 %copy-start = (f32[20,7680]{1,0:T(8,128)S(1)}, f32[20,7680]{1,0:T(8,128)}, u32[]{:S(2)}) copy-start(f32[20,7680]{1,0:T(8,128)} %param.11) | copy-start | bytes 1843204
  98.3 1.1 %copy-start.1 = (f32[20,7680]{1,0:T(8,128)}, f32[20,7680]{1,0:T(8,128)S(1)}, u32[]{:S(2)}) copy-start(f32[20,7680]{1,0:T(8,128)S(1)} %reshape.32) | copy-start | bytes 1843204

commit v3 on v2

--- a/solution.py
+++ b/solution.py
@@ -28,12 +28,12 @@
 
 def kernel(
     n, groups, heads, width,
-    q_in, k_in, v_in, step_in, w_in, gains,
+    kvq_in, step_in, w_in, fast_gain, window_gain,
     out, g_out, scale_out,
-    qb, kb, vb, stb, wb, wfull, kn, hid, tgt, gg, gu,
+    kv, qb, stb, wb, wfull, kn, hid, tgt, gg, gu,
     gstage, ginc, gsend, sums, sinc, scale_send, ostage,
-    s_in, r_q, r_k, r_v, r_st, r_w,
-    s_wf, s_kf, s_vf,
+    s_in, r_k, r_v, r_q, r_prior, r_st, r_w,
+    s_wf, s_kf,
     s_gp, r_gp, s_sp, r_sp, s_g, r_g, s_sc, r_sc, s_o, r_o,
 ):
     group = n // heads
@@ -76,8 +76,16 @@
     pending = []
     maybe = []
 
+    def flip_bits(value, bits):
+        for bit in (1, 2, 4):
+            if bits & bit:
+                value = value + bit - 2 * bit * lax.rem(value // bit, 2)
+        return value
+
+    order = range(heads)
+
     def spread(src_of, dst, recv, kind):
-        for step in range(heads):
+        for step in order:
             which = lax.rem(head + step, heads)
             device = which * group + block_member
             src = src_of(which)
@@ -114,16 +122,14 @@
         else:
             copy.start()
             pending.append(copy)
-    own = heads + block_slot
-    spread(lambda w: k_in.at[head_rows(w), :], kb.at[own], r_k.at[own], 0)
-    spread(lambda w: v_in.at[head_rows(w), :], vb.at[own], r_v.at[own], 1)
+    spread(lambda w: kvq_in.at[w, 0], kv.at[heads + block_slot, 0], r_k.at[block_slot], 0)
+    spread(lambda w: kvq_in.at[w, 1], kv.at[heads + block_slot, 1], r_v.at[block_slot], 1)
     spread(lambda w: step_in, stb.at[block_slot], r_st.at[block_slot], 2)
-    spread(lambda w: q_in.at[head_rows(w), :], qb.at[block_slot], r_q.at[block_slot], 3)
+    spread(lambda w: kvq_in.at[w, 2], qb.at[block_slot], r_q.at[block_slot], 3)
 
     @pl.when(member == 0)
     def _():
-        kb[:heads] = jnp.zeros((heads, width, LANES), BF16)
-        vb[:heads] = jnp.zeros((heads, width, LANES), BF16)
+        kv[:heads] = jnp.zeros((heads, 2, width, LANES), BF16)
 
     def landed(ref, sem):
         pltpu.make_async_copy(ref, ref, sem).wait()
@@ -145,14 +151,14 @@
 
     forwards = []
     for i in range(heads):
-        for buf, send, recv in ((kb, s_kf, r_k), (vb, s_vf, r_v)):
-            landed(buf.at[heads + i], recv.at[heads + i])
-            copy = remote(buf.at[heads + i], buf.at[i], send.at[i], recv.at[i], me + 1)
-            forwards.append(copy)
-
-            @pl.when(member < group - 1)
-            def _():
-                copy.start()
+        landed(kv.at[heads + i, 0], r_k.at[i])
+        landed(kv.at[heads + i, 1], r_v.at[i])
+        copy = remote(kv.at[heads + i], kv.at[i], s_kf.at[i], r_prior.at[i], me + 1)
+        forwards.append(copy)
+
+        @pl.when(member < group - 1)
+        def _():
+            copy.start()
     for d in range(group):
         for e in range(groups):
             if d + e == 0:
@@ -173,12 +179,12 @@
 
     for i in range(heads):
         there = pl.ds(i * LANES, LANES)
-        tgt[:, there] = (-stb[i, pl.ds(head, 1), :] * vb[heads + i].astype(F32)).astype(BF16)
+        tgt[:, there] = (-stb[i, pl.ds(head, 1), :] * kv[heads + i, 1].astype(F32)).astype(BF16)
     chunk = 2 * LANES
 
     def grad_chunk(c, carry):
         there = pl.ds(pl.multiple_of(c * chunk, chunk), chunk)
-        keys = jnp.concatenate([kb[heads + 2 * c], kb[heads + 2 * c + 1]], axis=1)
+        keys = jnp.concatenate([kv[heads + 2 * c, 0], kv[heads + 2 * c + 1, 0]], axis=1)
         gate = dot_tn(w1, keys) * scale
         up = dot_tn(w3, keys) * scale
         back = dot(w2, tgt[:, there]) * scale
@@ -190,7 +196,7 @@
         return carry
 
     lax.fori_loop(0, span // chunk, grad_chunk, 0)
-    own_keys = jnp.concatenate([kb[heads + i] for i in range(heads)], axis=1)
+    own_keys = jnp.concatenate([kv[heads + i, 0] for i in range(heads)], axis=1)
     for m, (left, right) in enumerate(((own_keys, gg), (own_keys, gu), (hid[...], tgt))):
         grad = dot_nt(left, right[...]) * scale
         for s in range(n):
@@ -207,12 +213,11 @@
     @pl.when(member > 0)
     def _():
         for i in range(heads):
-            landed(kb.at[i], r_k.at[i])
-            landed(vb.at[i], r_v.at[i])
+            landed(kv.at[i], r_prior.at[i])
 
     def flip(c, carry):
         at = pl.ds(pl.multiple_of(c * LANES, LANES), LANES)
-        kn[at, :] = kb[c].T
+        kn[at, :] = kv[c, 0].T
         return carry
 
     lax.fori_loop(0, 2 * heads, flip, 0)
@@ -245,6 +250,7 @@
         copy.start()
         pending.append(copy)
 
+
     for i in range(heads):
         landed(qb.at[i], r_q.at[i])
 
@@ -255,13 +261,20 @@
     in_window = (distance >= 0) & (distance < WINDOW)
     first_key = jnp.where(member == 0, span, 0)
 
+    def gain_column(ref):
+        return jnp.broadcast_to(ref[pl.ds(head, 1), :], (8, width)).T[:, 0:1]
+
+    fast_column = gain_column(fast_gain)
+    window_column = gain_column(window_gain)
+
     def normalize(field, gain):
         mean_sq = jnp.mean(field * field, axis=0, keepdims=True)
         return field * lax.rsqrt(mean_sq + 1e-05) * gain
 
     outs = []
 
-    def attend(c):
+    def attend(turn):
+        c = turn
         start = c * chunk
         query = jnp.concatenate([qb[2 * c], qb[2 * c + 1]], axis=1)
         scores = dot(kn[pl.ds(start, reach), :], query) * scale
@@ -269,13 +282,13 @@
         scores = jnp.where(allowed, scores, -1e30)
         weights = jnp.exp(scores - jnp.max(scores, axis=0, keepdims=True))
         probs = (weights / jnp.sum(weights, axis=0, keepdims=True)).astype(BF16)
-        values = jnp.concatenate([vb[2 * c + i] for i in range(reach // LANES)], axis=1)
+        values = jnp.concatenate([kv[2 * c + i, 1] for i in range(reach // LANES)], axis=1)
         attended = dot(values, probs)
-        window_part = normalize(attended, gains[1, :, 0:1])
+        window_part = normalize(attended, window_column)
         gate = dot_tn(w1, query) * scale
         up = dot_tn(w3, query) * scale
         hidden = (gate * jax.nn.sigmoid(gate) * up).astype(BF16)
-        fast_part = normalize(dot_tn(w2, hidden) * scale, gains[0, :, 0:1])
+        fast_part = normalize(dot_tn(w2, hidden) * scale, fast_column)
         result = (fast_part + window_part).astype(BF16)
         for half in range(2):
             i = 2 * c + half
@@ -344,6 +357,29 @@
             copy.wait_send()
 
 
+def prepare(heads, width, rows, k, v, q, weights, kvq, pieces, wide):
+    for m, ref in enumerate((k, v, q)):
+        flipped = ref[...].T
+        for h in range(heads):
+            kvq[h, m] = flipped[h * width : (h + 1) * width]
+    for h in range(heads):
+        for m in range(3):
+            at = (m * heads + h) * width
+            wide[h, m * rows : (m + 1) * rows, :] = weights[:, at : at + width]
+        pieces[h] = wide[h].astype(BF16)
+
+
+def finish(heads, width, rows, out_t, grads, scales, weights, layer_out, new_weights, momentum):
+    layer_out[...] = out_t[...].T
+    for h in range(heads):
+        grad = grads[h].astype(F32)
+        for m in range(3):
+            at = (m * heads + h) * width
+            part = grad[m * rows : (m + 1) * rows, :]
+            momentum[:, at : at + width] = part
+            new_weights[:, at : at + width] = (weights[:, at : at + width] - part) * scales[h, m : m + 1, :]
+
+
 def shards(queries, key_vectors, value_vectors, step_sizes, fast_weights, fast_gain, window_gain):
     tokens = queries.shape[0]
     heads = step_sizes.shape[1]
@@ -353,19 +389,21 @@
     group = n // heads
     rows = width // n
     assert tokens == LANES and heads * tokens == WINDOW
-    head = lax.axis_index("seq") // group
-    q_t, k_t, v_t = queries.T, key_vectors.T, value_vectors.T
-    pieces = (
-        fast_weights.astype(BF16).reshape(rows, 3, heads, width).transpose(2, 1, 0, 3)
-        .reshape(heads, 3 * rows, width)
-    )
-    gains = jnp.stack([fast_gain.reshape(heads, width), window_gain.reshape(heads, width)], axis=1)
-    gains = lax.dynamic_index_in_dim(gains, head, 0, keepdims=False)
-    gains = jnp.broadcast_to(gains[:, :, None], (2, width, LANES))
     span = heads * LANES
     vmem = pl.BlockSpec(memory_space=pltpu.VMEM)
     dma = pltpu.SemaphoreType.DMA
     more = max(group - 1, 1)
+    kvq, pieces = pl.pallas_call(
+        functools.partial(prepare, heads, width, rows),
+        out_shape=(
+            jax.ShapeDtypeStruct((heads, 3, width, LANES), BF16),
+            jax.ShapeDtypeStruct((heads, 3 * rows, width), BF16),
+        ),
+        in_specs=[vmem] * 4,
+        out_specs=(vmem, vmem),
+        scratch_shapes=[pltpu.VMEM((heads, 3 * rows, width), F32)],
+        name="prepare",
+    )(key_vectors, value_vectors, queries, fast_weights)
     out_t, grads, scales = pl.pallas_call(
         functools.partial(kernel, n, groups, heads, width),
         out_shape=(
@@ -373,12 +411,11 @@
             jax.ShapeDtypeStruct((heads, 3 * rows, width), BF16),
             jax.ShapeDtypeStruct((heads, 8, width), F32),
         ),
-        in_specs=[vmem] * 6,
+        in_specs=[vmem] * 5,
         out_specs=(vmem, vmem, vmem),
         scratch_shapes=[
+            pltpu.VMEM((2 * heads, 2, width, LANES), BF16),
             pltpu.VMEM((heads, width, LANES), BF16),
-            pltpu.VMEM((2 * heads, width, LANES), BF16),
-            pltpu.VMEM((2 * heads, width, LANES), BF16),
             pltpu.VMEM((heads, heads, LANES), F32),
             pltpu.VMEM((n, 3 * rows, width), BF16),
             pltpu.VMEM((3, width, width), F32),
@@ -394,8 +431,8 @@
             pltpu.VMEM((more, 8, width), F32),
             pltpu.VMEM((8, width), F32),
             pltpu.VMEM((heads, width, LANES), BF16),
-            dma((5, heads)), dma((heads,)), dma((2 * heads,)), dma((2 * heads,)), dma((heads,)), dma((n,)),
-            dma((heads // groups, groups * group)), dma((heads,)), dma((heads,)),
+            dma((5, heads)), dma((heads,)), dma((heads,)), dma((heads,)), dma((heads,)), dma((heads,)), dma((n,)),
+            dma((heads // groups, groups * group)), dma((heads,)),
             dma((more,)), dma((more,)), dma((more,)), dma((more,)),
             dma((heads,)), dma((heads,)), dma((heads,)), dma((heads,)), dma((heads,)), dma((heads,)),
         ],
@@ -403,14 +440,18 @@
             collective_id=0, has_side_effects=True, vmem_limit_bytes=60 << 20
         ),
         name="ttt",
-    )(q_t, k_t, v_t, step_sizes.T, pieces, gains)
-    layer_out = out_t.T
-    momentum = (
-        grads.astype(F32).reshape(heads, 3, rows, width).transpose(2, 1, 0, 3).reshape(rows, 3 * heads * width)
-    )
-    column_scale = scales[:, :3, :].transpose(1, 0, 2).reshape(1, -1)
-    new_weights = (fast_weights - momentum) * column_scale
-    return (layer_out, new_weights, momentum)
+    )(kvq, step_sizes.T, pieces, fast_gain.reshape(heads, width), window_gain.reshape(heads, width))
+    return pl.pallas_call(
+        functools.partial(finish, heads, width, rows),
+        out_shape=(
+            jax.ShapeDtypeStruct(queries.shape, BF16),
+            jax.ShapeDtypeStruct(fast_weights.shape, F32),
+            jax.ShapeDtypeStruct(fast_weights.shape, F32),
+        ),
+        in_specs=[vmem] * 4,
+        out_specs=(vmem, vmem, vmem),
+        name="finish",
+    )(out_t, grads, scales, fast_weights)
 
 
 def solution(mesh):

time: 99.9 us -> 95.8 us (0.959)
  local copies, waits for them, and re-layouts: 10.9 us -> 2.76 us
  Pallas kernels: 85.6 us -> 92.1 us
  other arithmetic: 2.2 us -> 0 us
    unnamed x22 -> x0, local copies, waits for them, and re-layouts: 8.15 us -> none
    pallas_call x0 -> x2, Pallas kernels: none -> 6.69 us  [the longest x1 3.67 us: shards(): pl.pallas_call(functools.partial(prepare, heads, width, rows), out_shape=...]
    reshape x5 -> x2, local copies, waits for them, and re-layouts: 1.55 us -> 2.76 us  [the longest x1 1.38 us: shards(): fast_gain.reshape(heads, width)]
    convert_element_type x1 -> x0, other arithmetic: 1.15 us -> none  [shards(): fast_weights.astype(BF16).reshape(rows, 3, heads, width)]
    mul x1 -> x0, other arithmetic: 1.04 us -> none  [shards(): new_weights = (fast_weights - momentum) * column_scale]
where the time goes in v3:
time: 95.8 us; the launch traced here: 95.5 us
  Pallas kernels  92.1 us (96%)
  local copies, waits for them, and re-layouts  2.76 us (3%)
    pallas_call x1, Pallas kernels, shards(): pl.pallas_call(functools.partial(kernel, n, groups, heads, width), out_sh...  85.4 us
    pallas_call x1, Pallas kernels, shards(): pl.pallas_call(functools.partial(prepare, heads, width, rows), out_shape=...  3.67 us
    pallas_call x1, Pallas kernels, shards(): pl.pallas_call(functools.partial(finish, heads, width, rows), out_shape=(...  3.02 us

profile of v3, /device:TPU:13, one launch (start us, length us, event | category | flops | bytes accessed | tf_op | source)
XLA Modules:
  0.0 95.5 jit_solution(3335570368128612209)
XLA Ops:
  0.6 1.4 %reshape.12.fast_gain = f32[8,320]{1,0:T(8,128)} reshape(f32[2560]{0:T(1024)} %param.12) | data formatting | bytes 20480 | tf_op jit(solution)/shard_map/reshape | solution.py:443
  2.0 1.4 %reshape.13.window_gain = f32[8,320]{1,0:T(8,128)} reshape(f32[2560]{0:T(1024)} %param.13) | data formatting | bytes 20480 | tf_op jit(solution)/shard_map/reshape | solution.py:443
  3.4 3.7 %prepare.1 = (bf16[8,3,320,128]{3,2,1,0:T(8,128)(2,1)}, bf16[8,60,320]{2,1,0:T(8,128)(2,1)}) custom-call(bf16[128,2560]{1,0:T(8,128)(2,1)} %k.1, bf16[128,2560]{1,0:T(8,128)(2,1)} %v.1, bf16[128,2560]{1,0:T(8,128)(2,1)} %q.1, f32[20,7680]{1,0:T(8,128)} %weights.3), custom_call_target="tpu_custom_call" | custom-call | tf_op jit(solution)/shard_map/prepare/pallas_call | solution.py:396
  7.1 85.4 %ttt.1 = (bf16[2560,128]{1,0:T(8,128)(2,1)}, bf16[8,60,320]{2,1,0:T(8,128)(2,1)}, f32[8,8,320]{2,1,0:T(8,128)}) custom-call(bf16[8,3,320,128]{3,2,1,0:T(8,128)(2,1)} %get-tuple-element.8.kvq_in, f32[8,128]{1,0:T(8,128)} %bitcast.1, bf16[8,60,320]{2,1,0:T(8,128)(2,1)} %get-tuple-element.9.w_in, f32[8,320]{1,0:T(8,128)} %reshape.12.fast_gain, ...), custom_call_target="tpu_custom_call" | custom-call | tf_op jit(solution)/shard_map/ttt/pallas_call | solution.py:407
  92.5 3.0 %finish.1 = (bf16[128,2560]{1,0:T(8,128)(2,1)}, f32[20,7680]{1,0:T(8,128)}, f32[20,7680]{1,0:T(8,128)}) custom-call(bf16[2560,128]{1,0:T(8,128)(2,1)} %get-tuple-element.10.out_t, bf16[8,60,320]{2,1,0:T(8,128)(2,1)} %get-tuple-element.11.grads, f32[8,8,320]{2,1,0:T(8,128)} %get-tuple-element.12.scales, f32[20,7680]{1,0:T(8,128)} %weights.3), custom_call_target="tpu_custom_call" | custom-call | tf_op jit(solution)/shard_map/finish/pallas_call | solution.py:444

commit v4 on v3

--- a/solution.py
+++ b/solution.py
@@ -31,7 +31,7 @@
     kvq_in, step_in, w_in, fast_gain, window_gain,
     out, g_out, scale_out,
     kv, qb, stb, wb, wfull, kn, hid, tgt, gg, gu,
-    gstage, ginc, gsend, sums, sinc, scale_send, ostage,
+    gstage, ginc, gsend, sums, sinc, scale_send, ostage, gain_rows,
     s_in, r_k, r_v, r_q, r_prior, r_st, r_w,
     s_wf, s_kf,
     s_gp, r_gp, s_sp, r_sp, s_g, r_g, s_sc, r_sc, s_o, r_o,
@@ -261,11 +261,15 @@
     in_window = (distance >= 0) & (distance < WINDOW)
     first_key = jnp.where(member == 0, span, 0)
 
-    def gain_column(ref):
-        return jnp.broadcast_to(ref[pl.ds(head, 1), :], (8, width)).T[:, 0:1]
-
-    fast_column = gain_column(fast_gain)
-    window_column = gain_column(window_gain)
+    for h in range(heads):
+        @pl.when(head == h)
+        def _():
+            at = slice(h * width, (h + 1) * width)
+            gain_rows[0] = jnp.broadcast_to(fast_gain[:, at], (8, width))
+            gain_rows[1] = jnp.broadcast_to(window_gain[:, at], (8, width))
+
+    fast_column = gain_rows[0].T[:, 0:1]
+    window_column = gain_rows[1].T[:, 0:1]
 
     def normalize(field, gain):
         mean_sq = jnp.mean(field * field, axis=0, keepdims=True)
@@ -431,6 +435,7 @@
             pltpu.VMEM((more, 8, width), F32),
             pltpu.VMEM((8, width), F32),
             pltpu.VMEM((heads, width, LANES), BF16),
+            pltpu.VMEM((2, 8, width), F32),
             dma((5, heads)), dma((heads,)), dma((heads,)), dma((heads,)), dma((heads,)), dma((heads,)), dma((n,)),
             dma((heads // groups, groups * group)), dma((heads,)),
             dma((more,)), dma((more,)), dma((more,)), dma((more,)),
@@ -440,7 +445,7 @@
             collective_id=0, has_side_effects=True, vmem_limit_bytes=60 << 20
         ),
         name="ttt",
-    )(kvq, step_sizes.T, pieces, fast_gain.reshape(heads, width), window_gain.reshape(heads, width))
+    )(kvq, step_sizes.T, pieces, fast_gain.reshape(1, -1), window_gain.reshape(1, -1))
     return pl.pallas_call(
         functools.partial(finish, heads, width, rows),
         out_shape=(

time: 95.8 us -> 95.8 us (level)
  no operation moved by 1% of the time
where the time goes in v4:
time: 95.8 us; the launch traced here: 95.5 us
  Pallas kernels  92.2 us (96%)
  local copies, waits for them, and re-layouts  2.63 us (3%)
    pallas_call x1, Pallas kernels, shards(): pl.pallas_call(functools.partial(kernel, n, groups, heads, width), out_sh...  85.6 us
    pallas_call x1, Pallas kernels, shards(): pl.pallas_call(functools.partial(prepare, heads, width, rows), out_shape=...  3.67 us
    pallas_call x1, Pallas kernels, shards(): pl.pallas_call(functools.partial(finish, heads, width, rows), out_shape=(...  3.02 us

profile of v4, /device:TPU:13, one launch (start us, length us, event | category | flops | bytes accessed | tf_op | source)
XLA Modules:
  0.0 95.5 jit_solution(1287670663363227447)
XLA Ops:
  0.6 1.3 %reshape.12.fast_gain = f32[1,2560]{1,0:T(1,128)} reshape(f32[2560]{0:T(1024)} %param.12) | data formatting | bytes 20480 | tf_op jit(solution)/shard_map/reshape | solution.py:448
  1.9 1.3 %reshape.13.window_gain = f32[1,2560]{1,0:T(1,128)} reshape(f32[2560]{0:T(1024)} %param.13) | data formatting | bytes 20480 | tf_op jit(solution)/shard_map/reshape | solution.py:448
  3.3 3.7 %prepare.1 = (bf16[8,3,320,128]{3,2,1,0:T(8,128)(2,1)}, bf16[8,60,320]{2,1,0:T(8,128)(2,1)}) custom-call(bf16[128,2560]{1,0:T(8,128)(2,1)} %k.1, bf16[128,2560]{1,0:T(8,128)(2,1)} %v.1, bf16[128,2560]{1,0:T(8,128)(2,1)} %q.1, f32[20,7680]{1,0:T(8,128)} %weights.3), custom_call_target="tpu_custom_call" | custom-call | tf_op jit(solution)/shard_map/prepare/pallas_call | solution.py:400
  6.9 85.6 %ttt.1 = (bf16[2560,128]{1,0:T(8,128)(2,1)}, bf16[8,60,320]{2,1,0:T(8,128)(2,1)}, f32[8,8,320]{2,1,0:T(8,128)}) custom-call(bf16[8,3,320,128]{3,2,1,0:T(8,128)(2,1)} %get-tuple-element.8.kvq_in, f32[8,128]{1,0:T(8,128)} %bitcast.1, bf16[8,60,320]{2,1,0:T(8,128)(2,1)} %get-tuple-element.9.w_in, f32[1,2560]{1,0:T(1,128)} %reshape.12.fast_gain, ...), custom_call_target="tpu_custom_call" | custom-call | tf_op jit(solution)/shard_map/ttt/pallas_call | solution.py:411
  92.5 3.0 %finish.1 = (bf16[128,2560]{1,0:T(8,128)(2,1)}, f32[20,7680]{1,0:T(8,128)}, f32[20,7680]{1,0:T(8,128)}) custom-call(bf16[2560,128]{1,0:T(8,128)(2,1)} %get-tuple-element.10.out_t, bf16[8,60,320]{2,1,0:T(8,128)(2,1)} %get-tuple-element.11.grads, f32[8,8,320]{2,1,0:T(8,128)} %get-tuple-element.12.scales, f32[20,7680]{1,0:T(8,128)} %weights.3), custom_call_target="tpu_custom_call" | custom-call | tf_op jit(solution)/shard_map/finish/pallas_call | solution.py:449
